TPU v7x, 32 devices: a whole 2x2x4 slice. The times are simulated.
32 devices in a mesh: seq: 4 (over x, core), fsdp: 8 (over z, y).
Axes of the slice: x: 2, y: 2, z: 4, core: 2. Of those that a mesh axis runs over, the one named last changes fastest.
Arguments:
- tokens: bfloat16 [2, 8, 1024, 1024], P(None, 'fsdp', 'seq'), may hold values from -6 to 6
- positions: int32 [2, 8, 1024], P(None, 'fsdp'), may hold values from 0 to 1023, as said below
- input_gain: bfloat16 [1024], P(('seq', 'fsdp')), may hold values from 0.5 to 1.5
- post_gain: bfloat16 [1024], P(('seq', 'fsdp')), may hold values from 0.5 to 1.5
- query_gain: bfloat16 [128], P(('seq', 'fsdp')), may hold values from 0.5 to 1.5
- key_gain: bfloat16 [128], P(('seq', 'fsdp')), may hold values from 0.5 to 1.5
- w_query: bfloat16 [1024, 2048], P(('seq', 'fsdp')), may hold values from -0.1875 to 0.1875
- w_key: bfloat16 [1024, 1024], P(('seq', 'fsdp')), may hold values from -0.1875 to 0.1875
- w_value: bfloat16 [1024, 1024], P(('seq', 'fsdp')), may hold values from -0.1875 to 0.1875
- w_out: bfloat16 [2048, 1024], P(('seq', 'fsdp')), may hold values from -1.5 to 1.5
- w_gate: bfloat16 [1024, 3072], P(('seq', 'fsdp')), may hold values from -0.1875 to 0.1875
- w_up: bfloat16 [1024, 3072], P(('seq', 'fsdp')), may hold values from -0.1875 to 0.1875
- w_down: bfloat16 [3072, 1024], P(('seq', 'fsdp')), may hold values from -0.109375 to 0.109375
- cotangent: bfloat16 [2, 8, 1024, 1024], P(None, 'fsdp', 'seq'), may hold values from -6 to 6
Outputs:
- block_out: bfloat16 [2, 8, 1024, 1024], P(None, 'fsdp', 'seq')
- tokens_grad: float32 [2, 8, 1024, 1024], P(None, 'fsdp', 'seq')
- input_gain_grad: float32 [1024], P(('seq', 'fsdp'))
- post_gain_grad: float32 [1024], P(('seq', 'fsdp'))
- query_gain_grad: float32 [128], P(('seq', 'fsdp'))
- key_gain_grad: float32 [128], P(('seq', 'fsdp'))
- w_query_grad: float32 [1024, 2048], P(('seq', 'fsdp'))
- w_key_grad: float32 [1024, 1024], P(('seq', 'fsdp'))
- w_value_grad: float32 [1024, 1024], P(('seq', 'fsdp'))
- w_out_grad: float32 [2048, 1024], P(('seq', 'fsdp'))
- w_gate_grad: float32 [1024, 3072], P(('seq', 'fsdp'))
- w_up_grad: float32 [1024, 3072], P(('seq', 'fsdp'))
- w_down_grad: float32 [3072, 1024], P(('seq', 'fsdp'))
Inputs may be any that keep to these rules, and one draw needn't show every extreme that they name: In each sequence the positions are a permutation of 0 to 1023 made of runs of 128 consecutive positions, each run starting at a multiple of 128; the order of the runs is drawn at random for each sequence.
All inputs are finite; a program needn't handle non-finite values.
Results may differ from a plain program's by a relative error of at most 0.02.
Values may be sent and summed in bfloat16 or wider, within the bound.
A program may use at most 160 MiB of HBM per device.

v0:
```python
import jax
import jax.numpy as jnp
from jax import lax
from jax.sharding import PartitionSpec as P

HEADS = 16
KV_HEADS = 8
HEAD_DIM = 128


EPSILON = 1e-06
ROPE_BASE = 1000000.0
NEGATIVE = -1e30


def inverse_root(values):
    return lax.rsqrt(jnp.mean(values * values, axis=-1, keepdims=True) + EPSILON)


def rope_tables(token_pos):
    half_width = HEAD_DIM // 2
    frequency = ROPE_BASE ** (-(jnp.arange(half_width, dtype=jnp.float32) * 2.0 / HEAD_DIM))
    angles = token_pos.astype(jnp.float32)[:, None] * frequency[None, :]
    cosine = jnp.cos(angles)
    sine = jnp.sin(angles)
    return (
        jnp.concatenate([cosine, cosine], axis=-1)[:, None, :],
        jnp.concatenate([sine, sine], axis=-1)[:, None, :],
    )


def rotate(values, cosine, sine):
    half_width = values.shape[-1] // 2
    turned = jnp.concatenate([-values[..., half_width:], values[..., :half_width]], axis=-1)
    return values * cosine + turned * sine


def rotate_back(grads, cosine, sine):
    half_width = grads.shape[-1] // 2
    scaled = grads * sine
    turned = jnp.concatenate([scaled[..., half_width:], -scaled[..., :half_width]], axis=-1)
    return grads * cosine + turned


def norm_back(grads, values, inverse, gain):
    scaled = grads * gain
    return inverse * scaled - values * inverse**3 * jnp.mean(
        scaled * values, axis=-1, keepdims=True
    )


def scores_of(queries, keys, query_pos, key_pos):
    block_rows = queries.shape[0]
    group = HEADS // KV_HEADS
    query_four = queries.reshape(block_rows, KV_HEADS, group, HEAD_DIM)
    key_three = keys.reshape(keys.shape[0], KV_HEADS, HEAD_DIM)
    raw = jnp.einsum(
        "qjgd,kjd->jgqk", query_four, key_three, preferred_element_type=jnp.float32
    ) * HEAD_DIM ** (-0.5)
    allowed = key_pos[None, :] <= query_pos[:, None]
    return (jnp.where(allowed, raw, NEGATIVE), query_four, key_three)


def attend(queries, keys, values, query_pos, key_pos):
    block_rows = queries.shape[0]
    scores, query_four, key_three = scores_of(queries, keys, query_pos, key_pos)
    top = jnp.max(scores, axis=-1, keepdims=True)
    exponent = jnp.exp(scores - top)
    total = jnp.sum(exponent, axis=-1, keepdims=True)
    soft_low = (exponent / total).astype(jnp.bfloat16)
    value_three = values.reshape(values.shape[0], KV_HEADS, HEAD_DIM)
    mixed = jnp.einsum("jgqk,kjd->qjgd", soft_low, value_three, preferred_element_type=jnp.float32)
    return (mixed.reshape(block_rows, HEADS * HEAD_DIM), top + jnp.log(total))


def attend_back(queries, keys, values, log_total, d_mixed, query_pos, key_pos):
    block_rows = queries.shape[0]
    group = HEADS // KV_HEADS
    scores, query_four, key_three = scores_of(queries, keys, query_pos, key_pos)
    soft = jnp.exp(scores - log_total)
    value_three = values.reshape(values.shape[0], KV_HEADS, HEAD_DIM)
    grad_four = d_mixed.reshape(block_rows, KV_HEADS, group, HEAD_DIM)
    d_soft = jnp.einsum(
        "qjgd,kjd->jgqk", grad_four, value_three, preferred_element_type=jnp.float32
    )
    d_scores = (soft * (d_soft - jnp.sum(d_soft * soft, axis=-1, keepdims=True))).astype(
        jnp.bfloat16
    )
    factor = HEAD_DIM ** (-0.5)
    d_queries = (
        jnp.einsum("jgqk,kjd->qjgd", d_scores, key_three, preferred_element_type=jnp.float32)
        * factor
    )
    d_keys = (
        jnp.einsum("jgqk,qjgd->kjd", d_scores, query_four, preferred_element_type=jnp.float32)
        * factor
    )
    d_values = jnp.einsum(
        "jgqk,qjgd->kjd", soft.astype(jnp.bfloat16), grad_four, preferred_element_type=jnp.float32
    )
    key_rows = keys.shape[0]
    return (
        d_queries.reshape(block_rows, HEADS, HEAD_DIM),
        d_keys.reshape(key_rows, KV_HEADS * HEAD_DIM),
        d_values.reshape(key_rows, KV_HEADS * HEAD_DIM),
    )


def body(
    tokens,
    positions,
    input_gain,
    post_gain,
    query_gain,
    key_gain,
    w_query,
    w_key,
    w_value,
    w_out,
    w_gate,
    w_up,
    w_down,
    cotangent,
):
    shards = (
        input_gain,
        post_gain,
        query_gain,
        key_gain,
        w_query,
        w_key,
        w_value,
        w_out,
        w_gate,
        w_up,
        w_down,
    )

    def fetch_weights():
        gathered = (
            lax.all_gather(shards[0], ("seq", "fsdp"), axis=0, tiled=True),
            lax.all_gather(shards[1], ("seq", "fsdp"), axis=0, tiled=True),
            lax.all_gather(shards[2], ("seq", "fsdp"), axis=0, tiled=True),
            lax.all_gather(shards[3], ("seq", "fsdp"), axis=0, tiled=True),
            lax.all_gather(shards[4], ("seq", "fsdp"), axis=0, tiled=True),
            lax.all_gather(shards[5], ("seq", "fsdp"), axis=0, tiled=True),
            lax.all_gather(shards[6], ("seq", "fsdp"), axis=0, tiled=True),
            lax.all_gather(shards[7], ("seq", "fsdp"), axis=0, tiled=True),
            lax.all_gather(shards[8], ("seq", "fsdp"), axis=0, tiled=True),
            lax.all_gather(shards[9], ("seq", "fsdp"), axis=0, tiled=True),
            lax.all_gather(shards[10], ("seq", "fsdp"), axis=0, tiled=True),
        )
        return gathered

    micro = tokens.shape[0]
    block_rows = tokens.shape[2]
    kv_width = KV_HEADS * HEAD_DIM
    first_row = lax.axis_index("seq") * block_rows
    saved = []
    results = []
    for batch_index in range(micro):
        gathered = fetch_weights()
        gain_in = gathered[0].astype(jnp.float32)
        gain_post = gathered[1].astype(jnp.float32)
        gain_query = gathered[2].astype(jnp.float32)
        gain_key = gathered[3].astype(jnp.float32)
        inputs = tokens[batch_index, 0].astype(jnp.float32)
        key_pos = positions[batch_index, 0]
        query_pos = lax.dynamic_slice_in_dim(key_pos, first_row, block_rows)
        cosine, sine = rope_tables(query_pos)
        inv_in = inverse_root(inputs)
        normed = (inputs * inv_in * gain_in).astype(jnp.bfloat16)
        q_raw = jnp.dot(normed, gathered[4], preferred_element_type=jnp.float32).reshape(
            block_rows, HEADS, HEAD_DIM
        )
        k_raw = jnp.dot(normed, gathered[5], preferred_element_type=jnp.float32).reshape(
            block_rows, KV_HEADS, HEAD_DIM
        )
        value_low = jnp.dot(normed, gathered[6], preferred_element_type=jnp.float32).astype(
            jnp.bfloat16
        )
        inv_query = inverse_root(q_raw)
        inv_key = inverse_root(k_raw)
        query_low = rotate(q_raw * inv_query * gain_query, cosine, sine).astype(jnp.bfloat16)
        key_low = (
            rotate(k_raw * inv_key * gain_key, cosine, sine)
            .astype(jnp.bfloat16)
            .reshape(block_rows, kv_width)
        )
        all_keys, all_values = (
            lax.all_gather(key_low, "seq", axis=0, tiled=True),
            lax.all_gather(value_low, "seq", axis=0, tiled=True),
        )
        mixed, log_total = attend(query_low, all_keys, all_values, query_pos, key_pos)
        mixed_low = mixed.astype(jnp.bfloat16)
        resid = inputs + jnp.dot(mixed_low, gathered[7], preferred_element_type=jnp.float32)
        inv_post = inverse_root(resid)
        post = (resid * inv_post * gain_post).astype(jnp.bfloat16)
        gate = jnp.dot(post, gathered[8], preferred_element_type=jnp.float32)
        upper = jnp.dot(post, gathered[9], preferred_element_type=jnp.float32)
        hidden = (jax.nn.silu(gate) * upper).astype(jnp.bfloat16)
        results.append(
            (resid + jnp.dot(hidden, gathered[10], preferred_element_type=jnp.float32)).astype(
                jnp.bfloat16
            )
        )
        saved.append(
            (
                inputs,
                inv_in,
                normed,
                q_raw,
                inv_query,
                k_raw,
                inv_key,
                query_low,
                all_keys,
                all_values,
                log_total,
                mixed_low,
                resid,
                inv_post,
                post,
                gate,
                upper,
                hidden,
                query_pos,
                key_pos,
                cosine,
                sine,
            )
        )
    totals = [jnp.zeros(item.shape, jnp.float32) for item in shards]
    totals = None
    input_grads = []
    for batch_index in range(micro):
        gathered = fetch_weights()
        if totals is None:
            totals = [jnp.zeros(item.shape, jnp.float32) for item in gathered]
        gain_in = gathered[0].astype(jnp.float32)
        gain_post = gathered[1].astype(jnp.float32)
        gain_query = gathered[2].astype(jnp.float32)
        gain_key = gathered[3].astype(jnp.float32)
        (
            inputs,
            inv_in,
            normed,
            q_raw,
            inv_query,
            k_raw,
            inv_key,
            query_low,
            all_keys,
            all_values,
            log_total,
            mixed_low,
            resid,
            inv_post,
            post,
            gate,
            upper,
            hidden,
            query_pos,
            key_pos,
            cosine,
            sine,
        ) = saved[batch_index]
        back_low = cotangent[batch_index, 0]
        back_full = back_low.astype(jnp.float32)
        totals[10] = totals[10] + jnp.einsum(
            "tf,td->fd", hidden, back_low, preferred_element_type=jnp.float32
        )
        d_hidden = jnp.einsum(
            "td,fd->tf", back_low, gathered[10], preferred_element_type=jnp.float32
        )
        sigma = jax.nn.sigmoid(gate)
        d_gate = (d_hidden * upper * sigma * (1.0 + gate * (1.0 - sigma))).astype(jnp.bfloat16)
        d_upper = (d_hidden * gate * sigma).astype(jnp.bfloat16)
        totals[8] = totals[8] + jnp.einsum(
            "td,tf->df", post, d_gate, preferred_element_type=jnp.float32
        )
        totals[9] = totals[9] + jnp.einsum(
            "td,tf->df", post, d_upper, preferred_element_type=jnp.float32
        )
        d_post = jnp.einsum("tf,df->td", d_gate, gathered[8], preferred_element_type=jnp.float32)
        d_post = d_post + jnp.einsum(
            "tf,df->td", d_upper, gathered[9], preferred_element_type=jnp.float32
        )
        totals[1] = totals[1] + jnp.sum(d_post * resid * inv_post, axis=0)
        d_resid = back_full + norm_back(d_post, resid, inv_post, gain_post)
        d_attn = d_resid.astype(jnp.bfloat16)
        totals[7] = totals[7] + jnp.einsum(
            "th,td->hd", mixed_low, d_attn, preferred_element_type=jnp.float32
        )
        d_mixed = jnp.einsum(
            "td,hd->th", d_attn, gathered[7], preferred_element_type=jnp.float32
        ).astype(jnp.bfloat16)
        d_queries, d_keys, d_values = attend_back(
            query_low, all_keys, all_values, log_total, d_mixed, query_pos, key_pos
        )
        key_part, value_part = (
            lax.psum_scatter(
                d_keys.astype(jnp.bfloat16), "seq", scatter_dimension=0, tiled=True
            ).astype(jnp.float32),
            lax.psum_scatter(
                d_values.astype(jnp.bfloat16), "seq", scatter_dimension=0, tiled=True
            ).astype(jnp.float32),
        )
        d_value_low = value_part.astype(jnp.bfloat16)
        key_turn = rotate_back(key_part.reshape(block_rows, KV_HEADS, HEAD_DIM), cosine, sine)
        query_turn = rotate_back(d_queries, cosine, sine)
        totals[3] = totals[3] + jnp.sum(key_turn * k_raw * inv_key, axis=(0, 1))
        totals[2] = totals[2] + jnp.sum(query_turn * q_raw * inv_query, axis=(0, 1))
        d_key_low = (
            norm_back(key_turn, k_raw, inv_key, gain_key)
            .reshape(block_rows, kv_width)
            .astype(jnp.bfloat16)
        )
        d_query_low = (
            norm_back(query_turn, q_raw, inv_query, gain_query)
            .reshape(block_rows, HEADS * HEAD_DIM)
            .astype(jnp.bfloat16)
        )
        totals[4] = totals[4] + jnp.einsum(
            "td,tf->df", normed, d_query_low, preferred_element_type=jnp.float32
        )
        totals[5] = totals[5] + jnp.einsum(
            "td,tf->df", normed, d_key_low, preferred_element_type=jnp.float32
        )
        totals[6] = totals[6] + jnp.einsum(
            "td,tf->df", normed, d_value_low, preferred_element_type=jnp.float32
        )
        d_normed = jnp.einsum(
            "tf,df->td", d_query_low, gathered[4], preferred_element_type=jnp.float32
        )
        d_normed = d_normed + jnp.einsum(
            "tf,df->td", d_key_low, gathered[5], preferred_element_type=jnp.float32
        )
        d_normed = d_normed + jnp.einsum(
            "tf,df->td", d_value_low, gathered[6], preferred_element_type=jnp.float32
        )
        totals[0] = totals[0] + jnp.sum(d_normed * inputs * inv_in, axis=0)
        input_grads.append(d_resid + norm_back(d_normed, inputs, inv_in, gain_in))
    owned = (
        lax.psum_scatter(totals[0], ("seq", "fsdp"), scatter_dimension=0, tiled=True),
        lax.psum_scatter(totals[1], ("seq", "fsdp"), scatter_dimension=0, tiled=True),
        lax.psum_scatter(totals[2], ("seq", "fsdp"), scatter_dimension=0, tiled=True),
        lax.psum_scatter(totals[3], ("seq", "fsdp"), scatter_dimension=0, tiled=True),
        lax.psum_scatter(totals[4], ("seq", "fsdp"), scatter_dimension=0, tiled=True),
        lax.psum_scatter(totals[5], ("seq", "fsdp"), scatter_dimension=0, tiled=True),
        lax.psum_scatter(totals[6], ("seq", "fsdp"), scatter_dimension=0, tiled=True),
        lax.psum_scatter(totals[7], ("seq", "fsdp"), scatter_dimension=0, tiled=True),
        lax.psum_scatter(totals[8], ("seq", "fsdp"), scatter_dimension=0, tiled=True),
        lax.psum_scatter(totals[9], ("seq", "fsdp"), scatter_dimension=0, tiled=True),
        lax.psum_scatter(totals[10], ("seq", "fsdp"), scatter_dimension=0, tiled=True),
    )
    block_out = jnp.stack(results)[:, None]
    tokens_grad = jnp.stack(input_grads)[:, None]
    return (
        block_out,
        tokens_grad,
        owned[0],
        owned[1],
        owned[2],
        owned[3],
        owned[4],
        owned[5],
        owned[6],
        owned[7],
        owned[8],
        owned[9],
        owned[10],
    )


def solution(mesh):
    placed = (
        P(None, "fsdp", "seq", None),
        P(None, "fsdp", None),
        P(("seq", "fsdp")),
        P(("seq", "fsdp")),
        P(("seq", "fsdp")),
        P(("seq", "fsdp")),
        P(("seq", "fsdp"), None),
        P(("seq", "fsdp"), None),
        P(("seq", "fsdp"), None),
        P(("seq", "fsdp"), None),
        P(("seq", "fsdp"), None),
        P(("seq", "fsdp"), None),
        P(("seq", "fsdp"), None),
        P(None, "fsdp", "seq", None),
    )
    return jax.shard_map(
        body,
        mesh=mesh,
        in_specs=placed,
        out_specs=(
            P(None, "fsdp", "seq", None),
            P(None, "fsdp", "seq", None),
            P(("seq", "fsdp")),
            P(("seq", "fsdp")),
            P(("seq", "fsdp")),
            P(("seq", "fsdp")),
            P(("seq", "fsdp"), None),
            P(("seq", "fsdp"), None),
            P(("seq", "fsdp"), None),
            P(("seq", "fsdp"), None),
            P(("seq", "fsdp"), None),
            P(("seq", "fsdp"), None),
            P(("seq", "fsdp"), None),
        ),
        check_vma=False,
    )
```

profile of v0, /device:TPU:0, one launch (start us, length us, event | category | flops | bytes accessed | tf_op | source)
XLA Modules:
  0.0 1912.9 jit_solution(4099556804375883768)
XLA Ops:
  12.1 42.0 %all-reduce.9 = (bf16[1024]{0:T(1024)(128)(2,1)S(1)}, bf16[128]{0:T(256)(128)(2,1)S(1)}, bf16[128]{0:T(256)(128)(2,1)S(1)}, bf16[1024]{0:T(1024)(128)(2,1)S(1)}) all-reduce(bf16[1024]{0:T(1024)(128)(2,1)S(1)} %dynamic-update-slice, bf16[128]{0:T(256)(128)(2,1)S(1)} %dynamic-update-slice.1, ...), channel_id=1, replica_groups=mesh['seq'=4,'fsdp'=8] {'seq','fsdp'}, use_global_device_ids=true, to_apply=%add | all-reduce | flops 2304 | bytes 9216
  56.3 14.0 all-gather.12.cloned.1.call-done
  76.8 51.9 %all-gather.16.cloned.1.call-done = bf16[1024,1024]{1,0:T(8,128)(2,1)} async-done(((bf16[32,1024]{1,0:T(8,128)(2,1)}), bf16[1024,1024]{1,0:T(8,128)(2,1)}) %all-gather.16.cloned.1.call-update) | async-done | bytes 2097168 | tf_op jit(solution)/shard_map/all_gather | solution.py:146
  143.6 8.2 all-gather.30.cloned.1.call-done
  155.3 20.5 %all-gather.14.cloned.1.call-done = bf16[1024,1024]{1,0:T(8,128)(2,1)} async-done(((bf16[256,1024]{1,0:T(8,128)(2,1)}), bf16[1024,1024]{1,0:T(8,128)(2,1)}) %all-gather.14.cloned.1.call-update) | async-done | bytes 2097168 | tf_op jit(solution)/shard_map/all_gather | solution.py:192
  179.4 61.5 %all-gather.20.cloned.1.call-done = bf16[1024,2048]{1,0:T(8,128)(2,1)} async-done(((bf16[32,2048]{1,0:T(8,128)(2,1)}), bf16[1024,2048]{1,0:T(8,128)(2,1)}) %all-gather.20.cloned.1.call-update) | async-done | bytes 4194320 | tf_op jit(solution)/shard_map/all_gather | solution.py:145
  264.2 9.1 fusion.134
  273.3 8.3 fusion.7
  289.2 40.2 %all-gather.22.cloned.1.call-done = bf16[2048,1024]{1,0:T(8,128)(2,1)} async-done(((bf16[64,1024]{1,0:T(8,128)(2,1)}), bf16[2048,1024]{1,0:T(8,128)(2,1)}) %all-gather.22.cloned.1.call-update) | async-done | bytes 4194320 | tf_op jit(solution)/shard_map/all_gather | solution.py:148
  334.7 17.7 all-gather.18.cloned.1.call-done
  352.4 9.2 fusion.135
  361.6 8.3 fusion.6
  379.4 45.5 %all-gather.26.cloned.1.call-done = bf16[1024,3072]{1,0:T(8,128)(2,1)} async-done(((bf16[32,3072]{1,0:T(8,128)(2,1)}), bf16[1024,3072]{1,0:T(8,128)(2,1)}) %all-gather.26.cloned.1.call-update) | async-done | bytes 6291472 | tf_op jit(solution)/shard_map/all_gather | solution.py:150
  431.0 64.6 %all-gather.24.cloned.1.call-done = bf16[1024,3072]{1,0:T(8,128)(2,1)} async-done(((bf16[32,3072]{1,0:T(8,128)(2,1)}), bf16[1024,3072]{1,0:T(8,128)(2,1)}) %all-gather.24.cloned.1.call-update) | async-done | bytes 6291472 | tf_op jit(solution)/shard_map/all_gather | solution.py:149
  501.9 64.7 %all-gather.28.cloned.1.call-done = bf16[3072,1024]{1,0:T(8,128)(2,1)} async-done(((bf16[96,1024]{1,0:T(8,128)(2,1)}), bf16[3072,1024]{1,0:T(8,128)(2,1)}) %all-gather.28.cloned.1.call-update) | async-done | bytes 6291472 | tf_op jit(solution)/shard_map/all_gather | solution.py:151
  566.6 9.2 multiply_convert_fusion.2
  591.8 9.8 multiply_convert_fusion
  616.7 10.0 bitcast_convert_fusion.1
  633.0 10.3 bitcast_convert_fusion
  643.4 11.7 fusion
  655.1 12.1 fusion.2
  671.7 11.9 fusion.3
  683.6 11.9 fusion.5
  709.1 15.8 reduce-scatter.16.cloned.1.call-done
  727.1 32.3 %reduce-scatter.12.cloned.1.call-done = bf16[256,1024]{0,1:T(8,128)(2,1)} async-done(((bf16[1024,1024]{0,1:T(8,128)(2,1)}), bf16[256,1024]{0,1:T(8,128)(2,1)}) %reduce-scatter.12.cloned.1.call-update) | async-done | bytes 524304 | tf_op jit(solution)/shard_map/reduce_scatter | solution.py:302
  857.9 41.5 %all-reduce.8 = (f32[1024]{0:T(1024)S(1)}, f32[1024]{0:T(1024)S(1)}, f32[128]{0:T(128)S(1)}, f32[128]{0:T(128)S(1)}) all-reduce(f32[1024]{0:T(1024)S(1)} %add.289, f32[1024]{0:T(1024)S(1)} %add.290, f32[128]{0:T(128)S(1)} %add.291, f32[128]{0:T(128)S(1)} %add.292), channel_id=6, replica_groups=mesh['seq'=4,'fsdp'=8] {'seq','fsdp'}, use_global_device_ids=true, to_apply=%region_28.29.clone | all-reduce | flops 2304 | bytes 18432
  906.6 144.1 %reduce-scatter.22.cloned.1.call-done = f32[32,1024]{1,0:T(8,128)} async-done(((f32[1024,1024]{1,0:T(8,128)}), f32[32,1024]{1,0:T(8,128)}) %reduce-scatter.22.cloned.1.call-update) | async-done | bytes 131088 | tf_op jit(solution)/shard_map/reduce_scatter | solution.py:350
  1050.8 184.0 %reduce-scatter.26.cloned.1.call-done = f32[64,1024]{1,0:T(8,128)} async-done(((f32[2048,1024]{1,0:T(8,128)}), f32[64,1024]{1,0:T(8,128)}) %reduce-scatter.26.cloned.1.call-update) | async-done | bytes 262160 | tf_op jit(solution)/shard_map/reduce_scatter | solution.py:352
  1234.7 161.6 %reduce-scatter.30.cloned.1.call-done = f32[32,3072]{1,0:T(8,128)} async-done(((f32[1024,3072]{1,0:T(8,128)}), f32[32,3072]{1,0:T(8,128)}) %reduce-scatter.30.cloned.1.call-update) | async-done | bytes 393232 | tf_op jit(solution)/shard_map/reduce_scatter | solution.py:354
  1396.3 162.0 %reduce-scatter.28.cloned.1.call-done = f32[32,3072]{1,0:T(8,128)} async-done(((f32[1024,3072]{1,0:T(8,128)}), f32[32,3072]{1,0:T(8,128)}) %reduce-scatter.28.cloned.1.call-update) | async-done | bytes 393232 | tf_op jit(solution)/shard_map/reduce_scatter | solution.py:353
  1558.3 161.1 %reduce-scatter.32.cloned.1.call-done = f32[96,1024]{1,0:T(8,128)} async-done(((f32[3072,1024]{1,0:T(8,128)}), f32[96,1024]{1,0:T(8,128)}) %reduce-scatter.32.cloned.1.call-update) | async-done | bytes 393232 | tf_op jit(solution)/shard_map/reduce_scatter | solution.py:355
  1719.4 186.4 %reduce-scatter.20.cloned.1.call-done = f32[32,2048]{1,0:T(8,128)} async-done(((f32[1024,2048]{1,0:T(8,128)}), f32[32,2048]{1,0:T(8,128)}) %reduce-scatter.20.cloned.1.call-update) | async-done | bytes 262160 | tf_op jit(solution)/shard_map/reduce_scatter | solution.py:349
  (398 shorter events, 255.5 us)
Async XLA Ops:
  7.2 63.1 %all-gather.12.cloned.1.call-start = ((), (), s32[]{:S(2)}) async-start(), calls=%async_computation.11 | async-start | bytes 2162688 | tf_op jit(solution)/shard_map/all_gather | solution.py:147
  7.9 120.8 %all-gather.16.cloned.1.call-start = ((), (), s32[]{:S(2)}) async-start(), calls=%async_computation.13 | async-start | bytes 2162688 | tf_op jit(solution)/shard_map/all_gather | solution.py:146
  8.7 143.1 %all-gather.30.cloned.1.call-start = ((), (), s32[]{:S(2)}) async-start(), calls=%async_computation.20 | async-start | bytes 2621440 | tf_op jit(solution)/shard_map/all_gather | solution.py:192
  54.2 197.6 %copy-start.75 = (f32[1024]{0:T(1024)}, f32[1024]{0:T(1024)S(1)}, u32[]{:S(2)}) copy-start(f32[1024]{0:T(1024)S(1)} %convert_element_type.258) | copy-start | bytes 12292
  56.3 191.4 %copy-start.91 = (f32[256]{0:T(256)}, f32[256]{0:T(256)S(1)}, u32[]{:S(2)}) copy-start(f32[256]{0:T(256)S(1)} %get-tuple-element.126) | copy-start | bytes 3076
  56.3 195.5 %copy-start.87 = (f32[256]{0:T(256)}, f32[256]{0:T(256)S(1)}, u32[]{:S(2)}) copy-start(f32[256]{0:T(256)S(1)} %get-tuple-element.169) | copy-start | bytes 3076
  73.8 102.0 %all-gather.14.cloned.1.call-start = ((), (), s32[]{:S(2)}) async-start(), calls=%async_computation.12 | async-start | bytes 2621440 | tf_op jit(solution)/shard_map/all_gather | solution.py:192
  75.5 165.3 %all-gather.20.cloned.1.call-start = ((), (), s32[]{:S(2)}) async-start(), calls=%async_computation.15 | async-start | bytes 4325376 | tf_op jit(solution)/shard_map/all_gather | solution.py:145
  76.1 188.1 %all-gather.32.cloned.1.call-start = ((), (), s32[]{:S(2)}) async-start(), calls=%async_computation.21 | async-start | bytes 2621440 | tf_op jit(solution)/shard_map/all_gather | solution.py:191
  76.8 180.0 %copy-start.39 = (f32[256,128]{0,1:T(8,128)}, f32[256,128]{0,1:T(8,128)S(1)}, u32[]{:S(2)}) copy-start(f32[256,128]{0,1:T(8,128)S(1)} %pad_maximum_fusion.2) | copy-start | bytes 393220
  76.8 180.0 %copy-start.58 = (f32[256,128]{0,1:T(8,128)}, f32[256,128]{0,1:T(8,128)S(1)}, u32[]{:S(2)}) copy-start(f32[256,128]{0,1:T(8,128)S(1)} %pad_maximum_fusion.3) | copy-start | bytes 393220
  139.0 190.4 %all-gather.22.cloned.1.call-start = ((), (), s32[]{:S(2)}) async-start(), calls=%async_computation.16 | async-start | bytes 4325376 | tf_op jit(solution)/shard_map/all_gather | solution.py:148
  139.8 212.6 %all-gather.18.cloned.1.call-start = ((), (), s32[]{:S(2)}) async-start(), calls=%async_computation.14 | async-start | bytes 2621440 | tf_op jit(solution)/shard_map/all_gather | solution.py:191
  139.9 194.4 %copy-start.41 = (f32[256,128]{0,1:T(8,128)}, f32[256,128]{0,1:T(8,128)S(1)}, u32[]{:S(2)}) copy-start(f32[256,128]{0,1:T(8,128)S(1)} %pad_maximum_fusion) | copy-start | bytes 393220
  139.9 194.4 %copy-start.60 = (f32[256,128]{0,1:T(8,128)}, f32[256,128]{0,1:T(8,128)S(1)}, u32[]{:S(2)}) copy-start(f32[256,128]{0,1:T(8,128)S(1)} %pad_maximum_fusion.1) | copy-start | bytes 393220
  141.0 283.9 %all-gather.26.cloned.1.call-start = ((), (), s32[]{:S(2)}) async-start(), calls=%async_computation.18 | async-start | bytes 6488064 | tf_op jit(solution)/shard_map/all_gather | solution.py:150
  141.7 353.9 %all-gather.24.cloned.1.call-start = ((), (), s32[]{:S(2)}) async-start(), calls=%async_computation.17 | async-start | bytes 6488064 | tf_op jit(solution)/shard_map/all_gather | solution.py:149
  142.3 424.3 %all-gather.28.cloned.1.call-start = ((), (), s32[]{:S(2)}) async-start(), calls=%async_computation.19 | async-start | bytes 6488064 | tf_op jit(solution)/shard_map/all_gather | solution.py:151
  143.1 556.7 %reduce-scatter.14.cloned.1.call-start = ((), (), s32[]{:S(2)}) async-start(), calls=%async_computation.23 | async-start | bytes 2621440 | tf_op jit(solution)/shard_map/reduce_scatter | solution.py:305
  143.1 111.5 %copy-start.96 = (f32[128]{0:T(128)}, f32[128]{0:T(128)S(1)}, u32[]{:S(2)}) copy-start(f32[128]{0:T(128)S(1)} %convert_element_type.267) | copy-start | bytes 1540
  379.1 230.9 %copy-start.20 = (f32[256,1024]{1,0:T(8,128)}, f32[256,1024]{1,0:T(8,128)S(1)}, u32[]{:S(2)}) copy-start(f32[256,1024]{1,0:T(8,128)S(1)} %get-tuple-element.159) | copy-start | bytes 3145732
  379.3 116.3 %copy-start.35 = (bf16[256,1024]{1,0:T(8,128)(2,1)}, bf16[256,1024]{1,0:T(8,128)(2,1)S(1)}, u32[]{:S(2)}) copy-start(bf16[256,1024]{1,0:T(8,128)(2,1)S(1)} %multiply_convert_fusion.7) | copy-start | bytes 1572868
  626.8 77.0 %reduce-scatter.18.cloned.1.call-start = ((), (), s32[]{:S(2)}) async-start(), calls=%async_computation.25 | async-start | bytes 2621440 | tf_op jit(solution)/shard_map/reduce_scatter | solution.py:305
  643.3 81.5 %reduce-scatter.16.cloned.1.call-start = ((), (), s32[]{:S(2)}) async-start(), calls=%async_computation.24 | async-start | bytes 2621440 | tf_op jit(solution)/shard_map/reduce_scatter | solution.py:302
  671.4 88.0 %reduce-scatter.12.cloned.1.call-start = ((), (), s32[]{:S(2)}) async-start(), calls=%async_computation.22 | async-start | bytes 2621440 | tf_op jit(solution)/shard_map/reduce_scatter | solution.py:302
  699.7 206.9 %reduce-scatter.24.cloned.1.call-start = ((), (), s32[]{:S(2)}) async-start(), calls=%async_computation.28 | async-start | bytes 4325376 | tf_op jit(solution)/shard_map/reduce_scatter | solution.py:351
  709.0 341.7 %reduce-scatter.22.cloned.1.call-start = ((), (), s32[]{:S(2)}) async-start(), calls=%async_computation.27 | async-start | bytes 4325376 | tf_op jit(solution)/shard_map/reduce_scatter | solution.py:350
  768.1 466.6 %reduce-scatter.26.cloned.1.call-start = ((), (), s32[]{:S(2)}) async-start(), calls=%async_computation.29 | async-start | bytes 8650752 | tf_op jit(solution)/shard_map/reduce_scatter | solution.py:352
  776.5 619.8 %reduce-scatter.30.cloned.1.call-start = ((), (), s32[]{:S(2)}) async-start(), calls=%async_computation.31 | async-start | bytes 12976128 | tf_op jit(solution)/shard_map/reduce_scatter | solution.py:354
  787.4 770.9 %reduce-scatter.28.cloned.1.call-start = ((), (), s32[]{:S(2)}) async-start(), calls=%async_computation.30 | async-start | bytes 12976128 | tf_op jit(solution)/shard_map/reduce_scatter | solution.py:353
  798.4 921.0 %reduce-scatter.32.cloned.1.call-start = ((), (), s32[]{:S(2)}) async-start(), calls=%async_computation.32 | async-start | bytes 12976128 | tf_op jit(solution)/shard_map/reduce_scatter | solution.py:355
  809.4 1096.4 %reduce-scatter.20.cloned.1.call-start = ((), (), s32[]{:S(2)}) async-start(), calls=%async_computation.26 | async-start | bytes 8650752 | tf_op jit(solution)/shard_map/reduce_scatter | solution.py:349
  (100 other events, 871.4 us)
Sparse Core Ops, SparseCore 0:
  11.0 59.2 all-gather.11
  73.3 55.3 all-gather.15
  130.3 21.4 all-gather.29
  153.2 22.5 all-gather.13
  178.7 62.0 all-gather.19
  242.8 21.3 all-gather.31
  267.3 62.0 all-gather.21
  331.0 21.3 all-gather.17
  355.3 69.5 all-gather.25
  427.6 67.9 all-gather.23
  498.6 67.9 all-gather.27
  626.9 29.8 reduce-scatter.13
  659.5 31.4 reduce-scatter.17
  693.4 31.4 reduce-scatter.15
  728.0 31.4 reduce-scatter.11
  762.1 144.4 reduce-scatter.23
  909.3 141.3 reduce-scatter.21
  1053.5 181.1 reduce-scatter.25
  1241.3 154.9 reduce-scatter.29
  1403.8 154.4 reduce-scatter.27
  1564.9 154.4 reduce-scatter.31
  1722.4 183.4 reduce-scatter.19
where the time goes:
time: 1920 us; the launch traced here: 1910 us
  waiting for transfers between devices  1450 us (76%)
  matrix products  250 us (13%)
  blocking collectives  83.5 us (4%)
  other arithmetic  70.3 us (4%)
  local copies, waits for them, and re-layouts  41.6 us (2%)
    reduce_scatter x1, waiting for transfers between devices, body(): lax.psum_scatter(totals[4], ('seq', 'fsdp'), scatter_dimension=0, tiled=T...  186 us
    reduce_scatter x1, waiting for transfers between devices, body(): lax.psum_scatter(totals[7], ('seq', 'fsdp'), scatter_dimension=0, tiled=T...  184 us
    reduce_scatter x1, waiting for transfers between devices, body(): lax.psum_scatter(totals[8], ('seq', 'fsdp'), scatter_dimension=0, tiled=T...  162 us
    reduce_scatter x1, waiting for transfers between devices, body(): lax.psum_scatter(totals[9], ('seq', 'fsdp'), scatter_dimension=0, tiled=T...  162 us
    reduce_scatter x1, waiting for transfers between devices, body(): lax.psum_scatter(totals[10], ('seq', 'fsdp'), scatter_dimension=0, tiled=...  161 us
    reduce_scatter x1, waiting for transfers between devices, body(): lax.psum_scatter(totals[5], ('seq', 'fsdp'), scatter_dimension=0, tiled=T...  144 us
    unnamed x2, blocking collectives  83.5 us
    all_gather x1, waiting for transfers between devices, fetch_weights(): lax.all_gather(shards[10], ('seq', 'fsdp'), axis=0, tiled=True)  64.7 us
  transfers between devices with their start and end apart: 22, of which 20 were waited for; matrix products, arithmetic and copies ran while one was open for 15% of the time, Pallas kernels for 0%

commit v1 on v0

v1 whole, which is shorter than its diff:
```python
import jax
import jax.numpy as jnp
from jax import lax
from jax.sharding import PartitionSpec as P

HEADS = 16
KV_HEADS = 8
HEAD_DIM = 128
EPSILON = 1e-06
ROPE_BASE = 1000000.0
NEGATIVE = -1e30
F32 = jnp.float32
BF16 = jnp.bfloat16


def inverse_root(values):
    return lax.rsqrt(jnp.mean(values * values, axis=-1, keepdims=True) + EPSILON)


def rope_tables(token_pos):
    half_width = HEAD_DIM // 2
    frequency = ROPE_BASE ** (-(jnp.arange(half_width, dtype=F32) * 2.0 / HEAD_DIM))
    angles = token_pos.astype(F32)[:, None] * frequency[None, :]
    cosine = jnp.cos(angles)
    sine = jnp.sin(angles)
    return (
        jnp.concatenate([cosine, cosine], axis=-1)[:, None, :],
        jnp.concatenate([sine, sine], axis=-1)[:, None, :],
    )


def rotate(values, cosine, sine):
    half_width = values.shape[-1] // 2
    turned = jnp.concatenate([-values[..., half_width:], values[..., :half_width]], axis=-1)
    return values * cosine + turned * sine


def rotate_back(grads, cosine, sine):
    half_width = grads.shape[-1] // 2
    scaled = grads * sine
    turned = jnp.concatenate([scaled[..., half_width:], -scaled[..., :half_width]], axis=-1)
    return grads * cosine + turned


def norm_back(grads, values, inverse, gain):
    scaled = grads * gain
    return inverse * scaled - values * inverse**3 * jnp.mean(
        scaled * values, axis=-1, keepdims=True
    )


def mul(eq, left, right):
    return jnp.einsum(eq, left, right, preferred_element_type=F32)


def sum_scatter(part, axis):
    return lax.psum_scatter(part.astype(BF16), axis, scatter_dimension=0, tiled=True).astype(F32)


def slice_weights(item, ways):
    rows = item.shape[0]
    return item.reshape(rows, ways, -1).transpose(1, 0, 2)


def plain_body(tokens, positions, g_in, g_post, g_query, g_key, w_query, w_key, w_value,
               w_out, w_gate, w_up, w_down, cotangent):
    ways = lax.axis_size("seq")
    heads, kv_heads = HEADS // ways, KV_HEADS // ways
    micro, rows, width = tokens.shape[0], tokens.shape[2], tokens.shape[3]
    length = positions.shape[2]
    everyone = ("seq", "fsdp")
    gains = [
        lax.all_gather(item, everyone, axis=0, tiled=True).astype(F32)
        for item in (g_in, g_post, g_query, g_key)
    ]
    gain_in, gain_post, gain_query, gain_key = gains

    def spread(*items):
        packed = jnp.concatenate([slice_weights(item, ways) for item in items], axis=2)
        packed = lax.all_to_all(packed, "seq", 0, 0, tiled=True)
        packed = lax.all_gather(packed, "fsdp", axis=1, tiled=True)
        packed = packed.reshape(-1, packed.shape[2])
        sizes = [item.shape[1] // ways for item in items]
        cuts = [sum(sizes[: at + 1]) for at in range(len(sizes) - 1)]
        return jnp.split(packed, cuts, axis=1)

    wq, wk, wv = spread(w_query, w_key, w_value)
    wo = lax.all_gather(w_out, "fsdp", axis=0, tiled=True)
    wg, wu = spread(w_gate, w_up)
    wd = lax.all_gather(w_down, "fsdp", axis=0, tiled=True)
    scale = HEAD_DIM ** (-0.5)

    def gather_rows(item):
        return lax.all_gather(item, "seq", axis=0, tiled=True)

    grads = None
    outs, token_grads = [], []
    for at in range(micro):
        inputs = tokens[at, 0].astype(F32)
        pos = positions[at, 0]
        cosine, sine = rope_tables(pos)
        allowed = pos[None, :] <= pos[:, None]
        inv_in = inverse_root(inputs)
        normed = gather_rows((inputs * inv_in * gain_in).astype(BF16))
        q_raw = mul("td,df->tf", normed, wq).reshape(length, heads, HEAD_DIM)
        k_raw = mul("td,df->tf", normed, wk).reshape(length, kv_heads, HEAD_DIM)
        value = mul("td,df->tf", normed, wv).astype(BF16).reshape(length, kv_heads, HEAD_DIM)
        inv_q, inv_k = inverse_root(q_raw), inverse_root(k_raw)
        query = rotate(q_raw * inv_q * gain_query, cosine, sine).astype(BF16)
        query = query.reshape(length, kv_heads, heads // kv_heads, HEAD_DIM)
        key = rotate(k_raw * inv_k * gain_key, cosine, sine).astype(BF16)
        scores = jnp.where(allowed, mul("qjgd,kjd->jgqk", query, key) * scale, NEGATIVE)
        soft = jax.nn.softmax(scores, axis=-1)
        soft_low = soft.astype(BF16)
        mixed = mul("jgqk,kjd->qjgd", soft_low, value).astype(BF16).reshape(length, -1)
        resid = inputs + sum_scatter(mul("th,hd->td", mixed, wo), "seq")
        inv_post = inverse_root(resid)
        post = gather_rows((resid * inv_post * gain_post).astype(BF16))
        gate = mul("td,df->tf", post, wg)
        upper = mul("td,df->tf", post, wu)
        sigma = jax.nn.sigmoid(gate)
        hidden = (gate * sigma * upper).astype(BF16)
        outs.append((resid + sum_scatter(mul("tf,fd->td", hidden, wd), "seq")).astype(BF16))
        back_low = cotangent[at, 0]
        back = gather_rows(back_low)
        g_down = mul("tf,td->fd", hidden, back)
        d_hidden = mul("td,fd->tf", back, wd)
        d_gate = (d_hidden * upper * sigma * (1.0 + gate * (1.0 - sigma))).astype(BF16)
        d_upper = (d_hidden * gate * sigma).astype(BF16)
        g_gate = mul("td,tf->df", post, d_gate)
        g_up = mul("td,tf->df", post, d_upper)
        d_post = sum_scatter(mul("tf,df->td", d_gate, wg) + mul("tf,df->td", d_upper, wu), "seq")
        post_grad = jnp.sum(d_post * resid * inv_post, axis=0)
        d_resid = back_low.astype(F32) + norm_back(d_post, resid, inv_post, gain_post)
        d_attn = gather_rows(d_resid.astype(BF16))
        g_out = mul("th,td->hd", mixed, d_attn)
        d_mixed = mul("td,hd->th", d_attn, wo).astype(BF16)
        d_mixed = d_mixed.reshape(length, kv_heads, heads // kv_heads, HEAD_DIM)
        d_soft = mul("qjgd,kjd->jgqk", d_mixed, value)
        d_scores = (soft * (d_soft - jnp.sum(d_soft * soft, axis=-1, keepdims=True))).astype(BF16)
        d_query = mul("jgqk,kjd->qjgd", d_scores, key) * scale
        d_key = mul("jgqk,qjgd->kjd", d_scores, query) * scale
        d_value = mul("jgqk,qjgd->kjd", soft_low, d_mixed).astype(BF16).reshape(length, -1)
        key_turn = rotate_back(d_key, cosine, sine)
        query_turn = rotate_back(d_query.reshape(length, heads, HEAD_DIM), cosine, sine)
        key_grad = jnp.sum(key_turn * k_raw * inv_k, axis=(0, 1))
        query_grad = jnp.sum(query_turn * q_raw * inv_q, axis=(0, 1))
        d_key = norm_back(key_turn, k_raw, inv_k, gain_key).astype(BF16).reshape(length, -1)
        d_query = norm_back(query_turn, q_raw, inv_q, gain_query).astype(BF16).reshape(length, -1)
        g_query_w = mul("td,tf->df", normed, d_query)
        g_key_w = mul("td,tf->df", normed, d_key)
        g_value_w = mul("td,tf->df", normed, d_value)
        d_normed = mul("tf,df->td", d_query, wq) + mul("tf,df->td", d_key, wk)
        d_normed = sum_scatter(d_normed + mul("tf,df->td", d_value, wv), "seq")
        in_grad = jnp.sum(d_normed * inputs * inv_in, axis=0)
        token_grads.append(d_resid + norm_back(d_normed, inputs, inv_in, gain_in))
        found = [in_grad, post_grad, query_grad, key_grad, g_query_w, g_key_w, g_value_w,
                 g_out, g_gate, g_up, g_down]
        grads = found if grads is None else [left + right for left, right in zip(grads, found)]

    small = [lax.psum_scatter(item, everyone, scatter_dimension=0, tiled=True) for item in grads[:4]]

    def columns_home(item):
        full, wide = item.shape
        item = item.reshape(ways, -1, wide).astype(BF16)
        item = lax.psum_scatter(item, "fsdp", scatter_dimension=1, tiled=True)
        item = lax.all_to_all(item, "seq", 0, 0, tiled=True)
        return item.transpose(1, 0, 2).reshape(item.shape[1], ways * wide).astype(F32)

    def rows_home(item):
        return sum_scatter(item, "fsdp")

    large = [columns_home(item) for item in grads[4:7]] + [rows_home(grads[7])]
    large += [columns_home(item) for item in grads[8:10]] + [rows_home(grads[10])]
    return (jnp.stack(outs)[:, None], jnp.stack(token_grads)[:, None], *small, *large)


def solution(mesh):
    both = ("seq", "fsdp")
    act = P(None, "fsdp", "seq", None)
    vec, mat = P(both), P(both, None)
    return jax.shard_map(
        plain_body,
        mesh=mesh,
        in_specs=(act, P(None, "fsdp", None), *[vec] * 4, *[mat] * 7, act),
        out_specs=(act, act, *[vec] * 4, *[mat] * 7),
        check_vma=False,
    )
```

time: 1920 us -> 1190 us (0.62)
  waiting for transfers between devices: 1450 us -> 713 us
  matrix products: 250 us -> 210 us
    reduce_scatter x11 -> x15, waiting for transfers between devices: 1050 us -> 499 us  [the longest x10 258 us: sum_scatter(): lax.psum_scatter(part.astype(BF16), axis, scatter_dimension=0, tiled=True)]
    all_gather x11 -> x12, waiting for transfers between devices: 396 us -> 201 us  [the longest x8 108 us: gather_rows(): return lax.all_gather(item, 'seq', axis=0, tiled=True)]
    dot_general x54 -> x52, matrix products: 250 us -> 186 us  [mul(): return jnp.einsum(eq, left, right, preferred_element_type=F32)]
    sub x0 -> x2, matrix products: none -> 23.6 us  [plain_body(): soft = jax.nn.softmax(scores, axis=-1)]
    all_to_all x0 -> x2, blocking collectives: none -> 19.9 us  [spread(): packed = lax.all_to_all(packed, 'seq', 0, 0, tiled=True)]
    convert_element_type x15 -> x16, other arithmetic: 29.6 us -> 41.2 us  [the longest x2 24.7 us: plain_body(): (soft * (d_soft - jnp.sum(d_soft * soft, axis=-1, keepdims=True))).astype...]
  transfers between devices with their start and end apart: 22 -> 32, of which waited for: 20 -> 24; matrix products, arithmetic and copies ran while one was open for 15% -> 25% of each run, Pallas kernels for 0% -> 0%
where the time goes in v1:
time: 1190 us; the launch traced here: 1180 us
  waiting for transfers between devices  713 us (60%)
  matrix products  210 us (18%)
  blocking collectives  100 us (8%)
  other arithmetic  88.3 us (7%)
  local copies, waits for them, and re-layouts  36.5 us (3%)
  starting transfers between devices  19.6 us (2%)
  between operations  16.6 us (1%)
    reduce_scatter x10, waiting for transfers between devices, sum_scatter(): lax.psum_scatter(part.astype(BF16), axis, scatter_dimension=0, tiled=True)  258 us
    reduce_scatter x5, waiting for transfers between devices, columns_home(): item = lax.psum_scatter(item, 'fsdp', scatter_dimension=1, tiled=True)  242 us
    dot_general x52, matrix products, mul(): return jnp.einsum(eq, left, right, preferred_element_type=F32)  186 us
    all_gather x8, waiting for transfers between devices, gather_rows(): return lax.all_gather(item, 'seq', axis=0, tiled=True)  108 us
    unnamed x2, blocking collectives  80.2 us
    all_gather x2, waiting for transfers between devices, spread(): packed = lax.all_gather(packed, 'fsdp', axis=1, tiled=True)  56.4 us
    all_gather x1, waiting for transfers between devices, plain_body(): wd = lax.all_gather(w_down, 'fsdp', axis=0, tiled=True)  37.3 us
    convert_element_type x2, other arithmetic, plain_body(): (soft * (d_soft - jnp.sum(d_soft * soft, axis=-1, keepdims=True))).astype...  24.7 us
  transfers between devices with their start and end apart: 32, of which 24 were waited for; matrix products, arithmetic and copies ran while one was open for 25% of the time, Pallas kernels for 0%

profile of v1, /device:TPU:0, one launch (start us, length us, event | category | flops | bytes accessed | tf_op | source)
XLA Modules:
  0.0 1184.2 jit_solution(1742899532645338715)
XLA Ops:
  10.3 10.0 all_to_all.35
  22.3 40.7 %all-reduce.9 = (bf16[1024]{0:T(1024)(128)(2,1)S(1)}, bf16[128]{0:T(256)(128)(2,1)S(1)}, bf16[128]{0:T(256)(128)(2,1)S(1)}, bf16[1024]{0:T(1024)(128)(2,1)S(1)}) all-reduce(bf16[1024]{0:T(1024)(128)(2,1)S(1)} %dynamic-update-slice, bf16[128]{0:T(256)(128)(2,1)S(1)} %dynamic-update-slice.1, ...), channel_id=1, replica_groups=mesh['seq'=4,'fsdp'=8] {'seq','fsdp'}, use_global_device_ids=true, to_apply=%add | all-reduce | flops 2304 | bytes 9216
  77.5 17.1 %all-gather.27.cloned.1.call-done = bf16[1024,1024]{1,0:T(8,128)(2,1)} async-done(((bf16[256,1024]{1,0:T(8,128)(2,1)}), bf16[1024,1024]{1,0:T(8,128)(2,1)}) %all-gather.27.cloned.1.call-update) | async-done | bytes 2097168 | tf_op jit(solution)/shard_map/all_gather | solution.py:94
  98.6 20.2 %all-gather.15.cloned.1.call-done = bf16[1024,1024]{1,0:T(8,128)(2,1)} async-done(((bf16[256,1024]{1,0:T(8,128)(2,1)}), bf16[1024,1024]{1,0:T(8,128)(2,1)}) %all-gather.15.cloned.1.call-update) | async-done | bytes 2097168 | tf_op jit(solution)/shard_map/all_gather | solution.py:94
  143.2 11.8 fusion.168
  175.3 11.9 %fusion.169 = (f32[2,2,1024]{2,1,0:T(2,128)S(1)}, f32[2,2,1024,1024]{2,3,1,0:T(8,128)}) fusion(pred[1024,1024]{0,1:T(8,128)(4,1)} %broadcast_compare_fusion, bf16[1024,2,128,1]{0,2,3,1:T(8,128)(2,1)} %get-tuple-element.212, bf16[1024,2,2,128]{0,3,2,1:T(8,128)(2,1)} %get-tuple-element.185), kind=kOutput, calls=%fused_computation.315 | convolution fusion | flops 1090520064 | bytes 19415040 | tf_op jit(solution)/shard_map/sub | solution.py:113
  199.5 9.8 all_to_all.36
  210.6 25.4 %reduce-scatter.20.cloned.1.call-done = bf16[256,1024]{1,0:T(8,128)(2,1)} async-done(((bf16[1024,1024]{1,0:T(8,128)(2,1)}), bf16[256,1024]{1,0:T(8,128)(2,1)}) %reduce-scatter.20.cloned.1.call-update) | async-done | bytes 524304 | tf_op jit(solution)/shard_map/reduce_scatter | solution.py:57
  242.9 56.4 %all-gather.23.cloned.1.call-done = bf16[4,256,1536]{2,0,1:T(4,128)(2,1)} async-done(((bf16[4,32,1536]{2,0,1:T(4,128)(2,1)}), bf16[4,256,1536]{2,0,1:T(4,128)(2,1)}) %all-gather.23.cloned.1.call-update) | async-done | bytes 3145744 | tf_op jit(solution)/shard_map/all_gather | solution.py:81
  303.4 18.6 %all-gather.29.cloned.1.call-done = bf16[1024,1024]{1,0:T(8,128)(2,1)} async-done(((bf16[256,1024]{1,0:T(8,128)(2,1)}), bf16[1024,1024]{1,0:T(8,128)(2,1)}) %all-gather.29.cloned.1.call-update) | async-done | bytes 2097168 | tf_op jit(solution)/shard_map/all_gather | solution.py:94
  331.1 37.3 %all-gather.25.cloned.1.call-done = bf16[768,1024]{1,0:T(8,128)(2,1)} async-done(((bf16[96,1024]{1,0:T(8,128)(2,1)}), bf16[768,1024]{1,0:T(8,128)(2,1)}) %all-gather.25.cloned.1.call-update) | async-done | bytes 1572880 | tf_op jit(solution)/shard_map/all_gather | solution.py:90
  368.4 22.8 %all-gather.37.cloned.1.call-done = bf16[1,1,1024,1024]{3,2,1,0:T(8,128)(2,1)} async-done(((bf16[1,1,256,1024]{3,2,1,0:T(8,128)(2,1)}), bf16[1,1,1024,1024]{3,2,1,0:T(8,128)(2,1)}) %all-gather.37.cloned.1.call-update) | async-done | bytes 2097168 | tf_op jit(solution)/shard_map/all_gather | solution.py:94
  404.6 10.8 all-gather.21.cloned.1.call-done
  424.6 14.9 %all-gather.35.cloned.1.call-done = bf16[1,1,1024,1024]{3,2,1,0:T(8,128)(2,1)} async-done(((bf16[1,1,256,1024]{3,2,1,0:T(8,128)(2,1)}), bf16[1,1,1024,1024]{3,2,1,0:T(8,128)(2,1)}) %all-gather.35.cloned.1.call-update) | async-done | bytes 2097168 | tf_op jit(solution)/shard_map/all_gather | solution.py:94
  457.7 15.7 %reduce-scatter.28.cloned.1.call-done = bf16[256,1024]{1,0:T(8,128)(2,1)} async-done(((bf16[1024,1024]{1,0:T(8,128)(2,1)}), bf16[256,1024]{1,0:T(8,128)(2,1)}) %reduce-scatter.28.cloned.1.call-update) | async-done | bytes 524304 | tf_op jit(solution)/shard_map/reduce_scatter | solution.py:57
  473.5 34.0 %reduce-scatter.24.cloned.1.call-done = bf16[256,1024]{1,0:T(8,128)(2,1)} async-done(((bf16[1024,1024]{1,0:T(8,128)(2,1)}), bf16[256,1024]{1,0:T(8,128)(2,1)}) %reduce-scatter.24.cloned.1.call-update) | async-done | bytes 524304 | tf_op jit(solution)/shard_map/reduce_scatter | solution.py:57
  510.2 31.1 %reduce-scatter.22.cloned.1.call-done = bf16[256,1024]{1,0:T(8,128)(2,1)} async-done(((bf16[1024,1024]{1,0:T(8,128)(2,1)}), bf16[256,1024]{1,0:T(8,128)(2,1)}) %reduce-scatter.22.cloned.1.call-update) | async-done | bytes 524304 | tf_op jit(solution)/shard_map/reduce_scatter | solution.py:57
  570.6 10.0 fusion.73
  580.7 8.2 fusion.5
  594.6 10.6 fusion.2
  605.2 12.2 %fusion.4 = bf16[2,2,1024,1024]{2,3,1,0:T(8,128)(2,1)S(1)} fusion(f32[2,1024,1024,2]{2,1,3,0:T(8,128)} %get-tuple-element.209, f32[2,2,1024]{2,1,0:T(2,128)S(1)} %get-tuple-element.208, f32[2,2,1024,1024]{2,3,1,0:T(8,128)} %get-tuple-element.203, f32[2,2,1024]{2,1,0:T(2,128)S(1)} %get-tuple-element.202), kind=kLoop, calls=%fused_computation.6 | loop fusion | flops 16777216 | bytes 41975808 | tf_op jit(solution)/shard_map/convert_element_type | solution.py:140
  624.6 12.4 %fusion.7 = bf16[2,2,1024,1024]{2,3,1,0:T(8,128)(2,1)S(1)} fusion(f32[2,1024,1024,2]{2,1,3,0:T(8,128)} %get-tuple-element.205, f32[2,2,1024]{2,1,0:T(2,128)S(1)} %get-tuple-element.204, f32[2,2,1024,1024]{2,3,1,0:T(8,128)} %get-tuple-element.201, f32[2,2,1024]{2,1,0:T(2,128)S(1)} %get-tuple-element.200), kind=kLoop, calls=%fused_computation.11 | loop fusion | flops 16777216 | bytes 41975808 | tf_op jit(solution)/shard_map/convert_element_type | solution.py:140
  648.3 8.9 fusion.70
  703.2 24.3 %reduce-scatter.44.cloned.1.call-done = bf16[96,1024]{1,0:T(8,128)(2,1)} async-done(((bf16[768,1024]{1,0:T(8,128)(2,1)}), bf16[96,1024]{1,0:T(8,128)(2,1)}) %reduce-scatter.44.cloned.1.call-update) | async-done | bytes 196624 | tf_op jit(solution)/shard_map/reduce_scatter | solution.py:57
  729.2 65.7 %reduce-scatter.40.cloned.1.call-done = bf16[4,32,768]{2,1,0:T(8,128)(2,1)} async-done(((bf16[4,256,768]{2,1,0:T(8,128)(2,1)}), bf16[4,32,768]{2,1,0:T(8,128)(2,1)}) %reduce-scatter.40.cloned.1.call-update) | async-done | bytes 196624 | tf_op jit(solution)/shard_map/reduce_scatter | solution.py:166
  804.5 55.2 %reduce-scatter.36.cloned.1.call-done = bf16[4,32,256]{2,1,0:T(8,128)(2,1)} async-done(((bf16[4,256,256]{2,1,0:T(8,128)(2,1)}), bf16[4,32,256]{2,1,0:T(8,128)(2,1)}) %reduce-scatter.36.cloned.1.call-update) | async-done | bytes 65552 | tf_op jit(solution)/shard_map/reduce_scatter | solution.py:166
  863.0 61.8 %reduce-scatter.34.cloned.1.call-done = bf16[4,32,256]{2,1,0:T(8,128)(2,1)} async-done(((bf16[4,256,256]{2,1,0:T(8,128)(2,1)}), bf16[4,32,256]{2,1,0:T(8,128)(2,1)}) %reduce-scatter.34.cloned.1.call-update) | async-done | bytes 65552 | tf_op jit(solution)/shard_map/reduce_scatter | solution.py:166
  932.2 58.9 %reduce-scatter.32.cloned.1.call-done = bf16[4,32,512]{2,1,0:T(8,128)(2,1)} async-done(((bf16[4,256,512]{2,1,0:T(8,128)(2,1)}), bf16[4,32,512]{2,1,0:T(8,128)(2,1)}) %reduce-scatter.32.cloned.1.call-update) | async-done | bytes 131088 | tf_op jit(solution)/shard_map/reduce_scatter | solution.py:166
  995.9 61.9 %reduce-scatter.38.cloned.1.call-done = bf16[64,1024]{1,0:T(8,128)(2,1)} async-done(((bf16[512,1024]{1,0:T(8,128)(2,1)}), bf16[64,1024]{1,0:T(8,128)(2,1)}) %reduce-scatter.38.cloned.1.call-update) | async-done | bytes 131088 | tf_op jit(solution)/shard_map/reduce_scatter | solution.py:57
  1060.1 30.6 %reduce-scatter.30.cloned.1.call-done = bf16[256,1024]{1,0:T(8,128)(2,1)} async-done(((bf16[1024,1024]{1,0:T(8,128)(2,1)}), bf16[256,1024]{1,0:T(8,128)(2,1)}) %reduce-scatter.30.cloned.1.call-update) | async-done | bytes 524304 | tf_op jit(solution)/shard_map/reduce_scatter | solution.py:57
  1090.8 34.6 %reduce-scatter.26.cloned.1.call-done = bf16[256,1024]{1,0:T(8,128)(2,1)} async-done(((bf16[1024,1024]{1,0:T(8,128)(2,1)}), bf16[256,1024]{1,0:T(8,128)(2,1)}) %reduce-scatter.26.cloned.1.call-update) | async-done | bytes 524304 | tf_op jit(solution)/shard_map/reduce_scatter | solution.py:57
  1127.5 39.5 %all-reduce.8 = (f32[1024]{0:T(1024)S(1)}, f32[1024]{0:T(1024)S(1)}, f32[128]{0:T(128)S(1)}, f32[128]{0:T(128)S(1)}) all-reduce(f32[1024]{0:T(1024)S(1)} %add.287, f32[1024]{0:T(1024)S(1)} %add.288, f32[128]{0:T(128)S(1)} %add.289, f32[128]{0:T(128)S(1)} %add.290), channel_id=12, replica_groups=mesh['seq'=4,'fsdp'=8] {'seq','fsdp'}, use_global_device_ids=true, to_apply=%region_32.33.clone | all-reduce | flops 2304 | bytes 18432
  (519 shorter events, 284.0 us)
Async XLA Ops:
  7.2 68.1 %all-gather.17.cloned.1.call-start = ((), (), s32[]{:S(2)}) async-start(), calls=%async_computation.23 | async-start | bytes 2359296 | tf_op jit(solution)/shard_map/all_gather | solution.py:81
  21.3 73.3 %all-gather.27.cloned.1.call-start = ((), (), s32[]{:S(2)}) async-start(), calls=%async_computation.30 | async-start | bytes 2621440 | tf_op jit(solution)/shard_map/all_gather | solution.py:94
  65.8 53.0 %all-gather.15.cloned.1.call-start = ((), (), s32[]{:S(2)}) async-start(), calls=%async_computation.22 | async-start | bytes 2621440 | tf_op jit(solution)/shard_map/all_gather | solution.py:94
  66.6 99.6 %all-gather.19.cloned.1.call-start = ((), (), s32[]{:S(2)}) async-start(), calls=%async_computation.24 | async-start | bytes 1179648 | tf_op jit(solution)/shard_map/all_gather | solution.py:88
  67.1 143.4 %reduce-scatter.16.cloned.1.call-start = ((), (), s32[]{:S(2)}) async-start(), calls=%async_computation.25 | async-start | bytes 2621440 | tf_op jit(solution)/shard_map/reduce_scatter | solution.py:57
  170.5 65.5 %reduce-scatter.20.cloned.1.call-start = ((), (), s32[]{:S(2)}) async-start(), calls=%async_computation.31 | async-start | bytes 2621440 | tf_op jit(solution)/shard_map/reduce_scatter | solution.py:57
  198.1 101.1 %all-gather.23.cloned.1.call-start = ((), (), s32[]{:S(2)}) async-start(), calls=%async_computation.27 | async-start | bytes 3538944 | tf_op jit(solution)/shard_map/all_gather | solution.py:81
  210.5 111.6 %all-gather.29.cloned.1.call-start = ((), (), s32[]{:S(2)}) async-start(), calls=%async_computation.32 | async-start | bytes 2621440 | tf_op jit(solution)/shard_map/all_gather | solution.py:94
  239.1 129.3 %all-gather.25.cloned.1.call-start = ((), (), s32[]{:S(2)}) async-start(), calls=%async_computation.28 | async-start | bytes 1769472 | tf_op jit(solution)/shard_map/all_gather | solution.py:90
  239.9 151.4 %all-gather.37.cloned.1.call-start = ((), (), s32[]{:S(2)}) async-start(), calls=%async_computation.48 | async-start | bytes 2621440 | tf_op jit(solution)/shard_map/all_gather | solution.py:94
  241.0 174.4 %all-gather.21.cloned.1.call-start = ((), (), s32[]{:S(2)}) async-start(), calls=%async_computation.26 | async-start | bytes 2621440 | tf_op jit(solution)/shard_map/all_gather | solution.py:94
  241.8 197.7 %all-gather.35.cloned.1.call-start = ((), (), s32[]{:S(2)}) async-start(), calls=%async_computation.47 | async-start | bytes 2621440 | tf_op jit(solution)/shard_map/all_gather | solution.py:94
  242.4 231.1 %reduce-scatter.28.cloned.1.call-start = ((), (), s32[]{:S(2)}) async-start(), calls=%async_computation.37 | async-start | bytes 2621440 | tf_op jit(solution)/shard_map/reduce_scatter | solution.py:57
  404.4 103.1 %reduce-scatter.24.cloned.1.call-start = ((), (), s32[]{:S(2)}) async-start(), calls=%async_computation.34 | async-start | bytes 2621440 | tf_op jit(solution)/shard_map/reduce_scatter | solution.py:57
  452.5 88.8 %reduce-scatter.22.cloned.1.call-start = ((), (), s32[]{:S(2)}) async-start(), calls=%async_computation.33 | async-start | bytes 2621440 | tf_op jit(solution)/shard_map/reduce_scatter | solution.py:57
  457.7 109.9 %all-gather.31.cloned.1.call-start = ((), (), s32[]{:S(2)}) async-start(), calls=%async_computation.35 | async-start | bytes 2621440 | tf_op jit(solution)/shard_map/all_gather | solution.py:94
  544.8 46.9 %all-gather.33.cloned.1.call-start = ((), (), s32[]{:S(2)}) async-start(), calls=%async_computation.38 | async-start | bytes 2621440 | tf_op jit(solution)/shard_map/all_gather | solution.py:94
  545.4 154.4 %reduce-scatter.42.cloned.1.call-start = ((), (), s32[]{:S(2)}) async-start(), calls=%async_computation.45 | async-start | bytes 1769472 | tf_op jit(solution)/shard_map/reduce_scatter | solution.py:166
  553.0 174.5 %reduce-scatter.44.cloned.1.call-start = ((), (), s32[]{:S(2)}) async-start(), calls=%async_computation.46 | async-start | bytes 1769472 | tf_op jit(solution)/shard_map/reduce_scatter | solution.py:57
  559.7 235.3 %reduce-scatter.40.cloned.1.call-start = ((), (), s32[]{:S(2)}) async-start(), calls=%async_computation.44 | async-start | bytes 1769472 | tf_op jit(solution)/shard_map/reduce_scatter | solution.py:166
  566.5 293.2 %reduce-scatter.36.cloned.1.call-start = ((), (), s32[]{:S(2)}) async-start(), calls=%async_computation.42 | async-start | bytes 589824 | tf_op jit(solution)/shard_map/reduce_scatter | solution.py:166
  658.8 266.0 %reduce-scatter.34.cloned.1.call-start = ((), (), s32[]{:S(2)}) async-start(), calls=%async_computation.41 | async-start | bytes 589824 | tf_op jit(solution)/shard_map/reduce_scatter | solution.py:166
  665.0 326.1 %reduce-scatter.32.cloned.1.call-start = ((), (), s32[]{:S(2)}) async-start(), calls=%async_computation.40 | async-start | bytes 1179648 | tf_op jit(solution)/shard_map/reduce_scatter | solution.py:166
  678.8 379.0 %reduce-scatter.38.cloned.1.call-start = ((), (), s32[]{:S(2)}) async-start(), calls=%async_computation.43 | async-start | bytes 1179648 | tf_op jit(solution)/shard_map/reduce_scatter | solution.py:57
  683.0 407.8 %reduce-scatter.30.cloned.1.call-start = ((), (), s32[]{:S(2)}) async-start(), calls=%async_computation.39 | async-start | bytes 2621440 | tf_op jit(solution)/shard_map/reduce_scatter | solution.py:57
  688.1 437.2 %reduce-scatter.26.cloned.1.call-start = ((), (), s32[]{:S(2)}) async-start(), calls=%async_computation.36 | async-start | bytes 2621440 | tf_op jit(solution)/shard_map/reduce_scatter | solution.py:57
  693.8 478.5 %reduce-scatter.18.cloned.1.call-start = ((), (), s32[]{:S(2)}) async-start(), calls=%async_computation.29 | async-start | bytes 2621440 | tf_op jit(solution)/shard_map/reduce_scatter | solution.py:57
  699.8 95.1 %all-to-all-start.6 = ((bf16[4,32,768]{2,1,0:T(8,128)(2,1)}), bf16[4,32,768]{2,1,0:T(8,128)(2,1)S(1)}, u32[]{:S(2)}, u32[]{:S(2)}) async-start(bf16[4,32,768]{2,1,0:T(8,128)(2,1)} %reduce-scatter.42.cloned.1.call-done), calls=%async_computation.20 | async-start | bytes 393216 | tf_op jit(solution)/shard_map/all_to_all | solution.py:167
  795.0 8.7 all-to-all-start.5
  859.7 65.1 %all-to-all-start.4 = ((bf16[4,32,256]{2,1,0:T(8,128)(2,1)}), bf16[4,32,256]{2,1,0:T(8,128)(2,1)S(1)}, u32[]{:S(2)}, u32[]{:S(2)}) async-start(bf16[4,32,256]{2,1,0:T(8,128)(2,1)} %reduce-scatter.36.cloned.1.call-done), calls=%async_computation.15 | async-start | bytes 131072 | tf_op jit(solution)/shard_map/all_to_all | solution.py:167
  924.8 7.4 all-to-all-start.3
  991.1 68.3 %all-to-all-start.2 = ((bf16[4,32,512]{2,1,0:T(8,128)(2,1)}), bf16[4,32,512]{2,1,0:T(8,128)(2,1)S(1)}, u32[]{:S(2)}, u32[]{:S(2)}) async-start(bf16[4,32,512]{2,1,0:T(8,128)(2,1)} %reduce-scatter.32.cloned.1.call-done), calls=%async_computation.11 | async-start | bytes 262144 | tf_op jit(solution)/shard_map/all_to_all | solution.py:167
  (146 other events, 5217.4 us)
Sparse Core Ops, SparseCore 0:
  21.4 50.4 all-gather.16
  73.5 21.0 all-gather.26
  96.2 22.5 all-gather.14
  120.8 40.1 all-gather.18
  170.6 31.4 reduce-scatter.15
  204.6 31.3 reduce-scatter.19
  238.7 60.4 all-gather.22
  300.8 21.1 all-gather.28
  324.2 44.1 all-gather.24
  369.9 21.3 all-gather.36
  392.8 22.5 all-gather.20
  416.9 22.5 all-gather.34
  442.0 31.4 reduce-scatter.27
  476.0 31.4 reduce-scatter.23
  509.9 31.3 reduce-scatter.21
  544.9 22.6 all-gather.30
  569.0 22.5 all-gather.32
  595.3 64.8 reduce-scatter.41
  663.7 63.8 reduce-scatter.43
  731.2 63.7 reduce-scatter.39
  798.3 61.3 reduce-scatter.35
  863.4 61.3 reduce-scatter.33
  928.2 62.8 reduce-scatter.31
  995.3 62.3 reduce-scatter.37
  1060.3 30.4 reduce-scatter.29
  1093.9 31.4 reduce-scatter.25
  1127.7 31.5 reduce-scatter.17

commit v2 on v1

--- a/solution.py
+++ b/solution.py
@@ -1,6 +1,10 @@
+import functools
+
 import jax
 import jax.numpy as jnp
 from jax import lax
+from jax.experimental import pallas as pl
+from jax.experimental.pallas import tpu as pltpu
 from jax.sharding import PartitionSpec as P
 
 HEADS = 16
@@ -175,12 +179,974 @@
     return (jnp.stack(outs)[:, None], jnp.stack(token_grads)[:, None], *small, *large)
 
 
+MESH = pl.DeviceIdType.MESH
+ANY = pl.ANY
+VMEM = pltpu.VMEM
+RUN = 128
+BLOCK = 256
+NARROW = (((1,), (1,)), ((), ()))
+TALL = (((0,), (0,)), ((), ()))
+PLAIN = (((1,), (0,)), ((), ()))
+LOG2E = 1.4426950408889634
+SCALE = HEAD_DIM ** (-0.5)
+VMEM_BYTES = 60 * 2**20
+
+
+def dot(left, right, dims=PLAIN):
+    return lax.dot_general(left, right, dims, preferred_element_type=F32)
+
+
+class Place:
+    def __init__(self, planes):
+        self.planes = planes
+        self.s = lax.axis_index("seq")
+        self.f = lax.axis_index("fsdp")
+        self.x, self.c = self.s // 2, self.s % 2
+        self.z, self.y = self.f // 2, self.f % 2
+        self.other_y = 1 - self.y
+        self.core_dev = (self.x * 2 + 1 - self.c, self.f)
+        self.x_dev = ((1 - self.x) * 2 + self.c, self.f)
+        self.far_dev = ((1 - self.x) * 2 + 1 - self.c, self.f)
+        self.y_dev = (self.s, self.z * 2 + self.other_y)
+
+    def z_at(self, step):
+        return lax.rem(self.z + step, self.planes)
+
+    def z_dev(self, step):
+        return (self.s, self.z_at(step) * 2 + self.y)
+
+    def peers(self):
+        return [self.core_dev, self.x_dev, self.far_dev, self.y_dev] + [
+            self.z_dev(step) for step in range(1, self.planes)
+        ]
+
+    def meet(self):
+        barrier = pltpu.get_barrier_semaphore()
+        for peer in self.peers():
+            pl.semaphore_signal(barrier, inc=1, device_id=peer, device_id_type=MESH)
+        pl.semaphore_wait(barrier, 3 + self.planes)
+
+
+def remote(src, dst, out_sem, in_sem, device):
+    return pltpu.make_async_remote_copy(
+        src_ref=src, dst_ref=dst, send_sem=out_sem, recv_sem=in_sem,
+        device_id=device, device_id_type=MESH,
+    )
+
+
+class Wire:
+    def __init__(self, out_sems, in_sems, own_sems):
+        self.out_sems, self.in_sems, self.own_sems = out_sems, in_sems, own_sems
+        self.sent, self.owned = [], 0
+
+    def send(self, src, dst, device):
+        at = len(self.sent)
+        copy = remote(src, dst, self.out_sems.at[at], self.in_sems.at[at], device)
+        copy.start()
+        self.sent.append(copy)
+        return copy
+
+    def own(self, src, dst):
+        copy = pltpu.make_async_copy(src, dst, self.own_sems.at[self.owned])
+        copy.start()
+        self.owned += 1
+        return copy
+
+    def close(self):
+        for copy in self.sent:
+            copy.wait_send()
+
+
+def wire_scratch(copies, owns):
+    return [
+        pltpu.SemaphoreType.DMA((copies,)),
+        pltpu.SemaphoreType.DMA((copies,)),
+        pltpu.SemaphoreType.DMA((owns,)),
+    ]
+
+
+class Reducer:
+    def __init__(self, place, part, core_out, core_in, x_out, x_in, keep, sems):
+        self.place, self.part = place, part
+        self.core_out, self.core_in = core_out, core_in
+        self.x_out, self.x_in, self.keep = x_out, x_in, keep
+        self.core_s, self.core_r, self.x_s, self.x_r = sems
+
+    def block(self, step):
+        p = self.place
+        turn = step % 4
+        x = jnp.where(turn % 2 == 0, 1 - p.x, p.x)
+        c = jnp.where(turn < 2, 1 - p.c, p.c)
+        return step // 4, x * 2 + c
+
+    def core_copy(self, slot):
+        return remote(self.core_out.at[slot], self.core_in.at[slot], self.core_s.at[slot],
+                      self.core_r.at[slot], self.place.core_dev)
+
+    def x_copy(self, micro):
+        return remote(self.x_out.at[micro], self.x_in.at[micro], self.x_s.at[micro],
+                      self.x_r.at[micro], self.place.x_dev)
+
+    def take(self, step, send_x=True):
+        micro, turn = step // 4, step % 4
+
+        @pl.when(turn < 2)
+        def _():
+            slot = micro * 2 + turn
+            self.core_out[slot] = self.part[...].astype(BF16)
+            self.core_copy(slot).start()
+
+        @pl.when(turn == 2)
+        def _():
+            slot = micro * 2
+            self.core_copy(slot).wait_recv()
+            self.x_out[micro] = (self.part[...] + self.core_in[slot].astype(F32)).astype(BF16)
+            if send_x:
+                self.x_copy(micro).start()
+
+        @pl.when(turn == 3)
+        def _():
+            slot = micro * 2 + 1
+            self.core_copy(slot).wait_recv()
+            self.keep[micro] = self.part[...] + self.core_in[slot].astype(F32)
+
+    def total(self, micro):
+        self.x_copy(micro).wait_recv()
+        return self.keep[micro] + self.x_in[micro].astype(F32)
+
+    def close(self, send_x=True):
+        for slot in range(4):
+            self.core_copy(slot).wait_send()
+        if send_x:
+            for micro in range(2):
+                self.x_copy(micro).wait_send()
+
+
+def reducer_scratch(width):
+    return [
+        VMEM((4, BLOCK, width), BF16),
+        VMEM((4, BLOCK, width), BF16),
+        VMEM((2, BLOCK, width), BF16),
+        VMEM((2, BLOCK, width), BF16),
+        VMEM((2, BLOCK, width), F32),
+        pltpu.SemaphoreType.DMA((4,)),
+        pltpu.SemaphoreType.DMA((4,)),
+        pltpu.SemaphoreType.DMA((2,)),
+        pltpu.SemaphoreType.DMA((2,)),
+    ]
+
+
+def row_mean(values):
+    return jnp.mean(values, axis=-1, keepdims=True)
+
+
+def spread_gain(table, row, devices, width):
+    per = width // devices
+    lanes = lax.broadcasted_iota(jnp.int32, (RUN, width), 0)
+    column = lax.broadcasted_iota(jnp.int32, (RUN, width), 1)
+    pick = (lanes == lax.rem(column, per)).astype(BF16)
+    picked = dot(table, pick)
+    rows = lax.broadcasted_iota(jnp.int32, (devices * 8, width), 0)
+    owner = lax.broadcasted_iota(jnp.int32, (devices * 8, width), 1) // per
+    return jnp.sum(jnp.where(rows == owner * 8 + row, picked, 0.0), axis=0, keepdims=True)
+
+
+def two_runs(ref, first, second):
+    return jnp.concatenate([ref[first], ref[second]], axis=0)
+
+
+def joined(value):
+    return value.reshape(-1, value.shape[-1])
+
+
+def flat(ref):
+    return joined(ref[...])
+
+
+def front_kernel(
+    planes,
+    order, rank, tokens, cotangent, gain_tile, cosine, sine,
+    s_q, s_k, s_v, s_o, s_g, s_u, s_d,
+    wq, wk, wv, wo, wg, wu, wd,
+    normed, query, key, value, q_unit, k_unit, roots, mixed, lse,
+    resid, post_full, back_full, gains,
+    tok_full, gain_all, post_own, part,
+    core_out, core_in, x_out, x_in, keep, core_s, core_r, x_s, x_r,
+    out_sems, in_sems, own_sems,
+):
+    p = Place(planes)
+    s, f = p.s, p.f
+    devices = 8 * planes
+    wire = Wire(out_sems, in_sems, own_sems)
+    reducer = Reducer(p, part, core_out, core_in, x_out, x_in, keep, (core_s, core_r, x_s, x_r))
+    rows = BLOCK
+    mine = pl.ds(s * rows, rows)
+    theirs = pl.ds(p.x_dev[0] * rows, rows)
+    length = 4 * rows
+    p.meet()
+
+    gain_all[s, f] = gain_tile[...]
+    gain_in = [wire.send(gain_all.at[s, f], gain_all.at[s, f], dev)
+               for dev in (p.core_dev, p.x_dev, p.far_dev)]
+
+    def spread_columns(item, full):
+        wide = item.shape[1] // 4
+        came = [wire.own(item.at[:, pl.ds(s * wide, wide)], full.at[s, f])]
+        sent = []
+        for dev in (p.core_dev, p.x_dev, p.far_dev):
+            sent.append(wire.send(item.at[:, pl.ds(dev[0] * wide, wide)], full.at[s, f], dev))
+        return came, sent
+
+    first = [spread_columns(item, full) for item, full in ((s_q, wq), (s_k, wk), (s_v, wv))]
+    tok_here, tok_x, tok_core = [], [], []
+    for micro in range(2):
+        to = tok_full.at[pl.ds(micro * (length // RUN) + s * 2, 2)]
+        tok_here.append(wire.own(tokens.at[micro], to))
+        tok_x.append(wire.send(tokens.at[micro], to, p.x_dev))
+        tok_core.append(wire.send(tokens.at[micro], to, p.core_dev))
+    second = [spread_columns(item, full) for item, full in ((s_g, wg), (s_u, wu))]
+
+    def arrived(group):
+        came, sent = group
+        for copy in came:
+            copy.wait()
+        for copy in sent:
+            copy.wait_recv()
+
+    def blocks(full, at):
+        return full.at[:, at] if len(full.shape) == 4 else full.at[at]
+
+    def push_planes(full):
+        here = blocks(full, f)
+        far = [wire.send(here, here, p.z_dev(step)) for step in range(1, planes)]
+        return far, [wire.send(here, here, p.y_dev)]
+
+    def forward(full, state):
+        far, side = state
+        for step, copy in enumerate(far, 1):
+            copy.wait_recv()
+            there = blocks(full, p.z_at(planes - step) * 2 + p.y)
+            side.append(wire.send(there, there, p.y_dev))
+
+    def settle(state):
+        for copy in state[1]:
+            copy.wait_recv()
+
+    def push_rows(item, full):
+        kept = wire.own(item, full.at[f])
+        far = [wire.send(item, full.at[f], p.z_dev(step)) for step in range(1, planes)]
+        return kept, (far, [wire.send(item, full.at[f], p.y_dev)])
+
+    for copy in gain_in:
+        copy.wait_recv()
+    gain_state = push_planes(gain_all)
+    states = []
+    for group, full in zip(first, (wq, wk, wv)):
+        arrived(group)
+        states.append(push_planes(full))
+    forward(gain_all, gain_state)
+    out_kept, out_state = push_rows(s_o, wo)
+    tok_fwd = []
+    for micro in range(2):
+        tok_x[micro].wait_recv()
+        block = tok_full.at[pl.ds(micro * (length // RUN) + p.x_dev[0] * 2, 2)]
+        tok_fwd.append(wire.send(block, block, p.core_dev))
+    for full, state in zip((wq, wk, wv), states):
+        forward(full, state)
+    back_x, back_core, back_kept = [], [], []
+    for micro in range(2):
+        to = back_full.at[micro, mine]
+        back_x.append(wire.send(cotangent.at[micro], to, p.x_dev))
+        back_kept.append(wire.own(cotangent.at[micro], to))
+        back_core.append(wire.send(cotangent.at[micro], to, p.core_dev))
+    wide_states = []
+    for group, full in zip(second, (wg, wu)):
+        arrived(group)
+        wide_states.append(push_planes(full))
+    down_kept, down_state = push_rows(s_d, wd)
+    settle(gain_state)
+    table = gain_all[...].reshape(devices * 8, RUN).astype(BF16)
+    gain_first = spread_gain(table, 0, devices, 1024)
+    gain_post = spread_gain(table, 1, devices, 1024)
+    gain_query = spread_gain(table, 2, devices, RUN)
+    gain_key = spread_gain(table, 3, devices, RUN)
+    gains[...] = jnp.zeros_like(gains)
+    gains[0:1] = gain_first
+    gains[1:2] = gain_post
+    gains[2:3, 0:RUN] = gain_query
+    gains[3:4, 0:RUN] = gain_key
+    for copy in tok_here:
+        copy.wait()
+    for copy in tok_core + tok_fwd:
+        copy.wait_recv()
+    for state in states:
+        settle(state)
+
+    def project(step, carry):
+        here = pl.ds(pl.multiple_of(step * BLOCK, BLOCK), BLOCK)
+        raw = two_runs(tok_full, order[step * 2], order[step * 2 + 1]).astype(F32)
+        root = lax.rsqrt(row_mean(raw * raw) + EPSILON)
+        low = (raw * root * gains[0:1]).astype(BF16)
+        normed[here] = low
+        turn = pl.ds(pl.multiple_of(lax.rem(step, length // BLOCK) * BLOCK, BLOCK), BLOCK)
+        cos, sin = cosine[turn], sine[turn]
+        found = []
+        for weight, low_ref, unit_ref, row in ((wq, query, q_unit, 2), (wk, key, k_unit, 3)):
+            product = dot(low, flat(weight))
+            gain = gains[row : row + 1, 0:RUN]
+            for head in range(low_ref.shape[1] // HEAD_DIM):
+                at = slice(head * HEAD_DIM, (head + 1) * HEAD_DIM)
+                one = product[:, at]
+                inverse = lax.rsqrt(row_mean(one * one) + EPSILON)
+                unit = one * inverse
+                unit_ref[here, at] = unit.astype(BF16)
+                scaled = unit * gain
+                low_ref[here, at] = (scaled * cos + pltpu.roll(scaled, HEAD_DIM // 2, 1) * sin).astype(BF16)
+                found.append(inverse)
+        for at, inverse in enumerate(found):
+            roots[here, at : at + 1] = inverse
+        value[here] = dot(low, flat(wv)).astype(BF16)
+        return carry
+
+    lax.fori_loop(0, 2 * length // BLOCK, project, 0)
+    for full, state in zip((wg, wu), wide_states):
+        forward(full, state)
+
+    def attend(step, carry):
+        micro, head = step // 2, lax.rem(step, 2)
+        keys_at = pl.ds(pl.multiple_of(head * HEAD_DIM, HEAD_DIM), HEAD_DIM)
+        lanes = [pl.ds(pl.multiple_of(head * 2 * HEAD_DIM + g * HEAD_DIM, HEAD_DIM), HEAD_DIM) for g in range(2)]
+        for block in range(length // BLOCK):
+            here = pl.ds(pl.multiple_of(micro * length + block * BLOCK, BLOCK), BLOCK)
+            seen = (block + 1) * BLOCK
+            past = pl.ds(pl.multiple_of(micro * length, BLOCK), seen)
+            asked = jnp.concatenate([query[here, lane] for lane in lanes], axis=0)
+            scores = dot(asked, key[past, keys_at], NARROW)
+            line = lax.broadcasted_iota(jnp.int32, (2 * BLOCK, seen), 0)
+            line = jnp.where(line >= BLOCK, line - BLOCK, line) + block * BLOCK
+            column = lax.broadcasted_iota(jnp.int32, (2 * BLOCK, seen), 1)
+            scores = jnp.where(column <= line, scores, NEGATIVE)
+            top = jnp.max(scores, axis=-1, keepdims=True)
+            weight = jnp.exp2((scores - top) * (SCALE * LOG2E))
+            total = jnp.sum(weight, axis=-1, keepdims=True)
+            out = dot(weight.astype(BF16), value[past, keys_at]) * (1.0 / total)
+            level = top * (SCALE * LOG2E) + jnp.log2(total)
+            for g, lane in enumerate(lanes):
+                half = slice(g * BLOCK, (g + 1) * BLOCK)
+                pair = pl.ds(micro * (length // RUN) + block * 2, 2)
+                mixed[pair, :, lane] = out[half].astype(BF16).reshape(2, RUN, HEAD_DIM)
+                lse[step, pl.ds(block * BLOCK, BLOCK), g : g + 1] = level[half]
+        return carry
+
+    lax.fori_loop(0, 2, attend, 0)
+    forward(wo, out_state)
+    forward(wd, down_state)
+    lax.fori_loop(2, 4, attend, 0)
+    for micro in range(2):
+        back_x[micro].wait_recv()
+        block = back_full.at[micro, theirs]
+        back_core.append(wire.send(block, block, p.core_dev))
+    out_kept.wait()
+    settle(out_state)
+
+    def mix_out(step, carry):
+        micro, block = reducer.block(step)
+        at = micro * (length // RUN) + block * 2
+        low = two_runs(mixed, rank[at], rank[at + 1])
+        part[...] = dot(low, flat(wo))
+        reducer.take(step)
+        return carry
+
+    lax.fori_loop(0, 8, mix_out, 0)
+    posts = []
+    for micro in range(2):
+        total = reducer.total(micro)
+        own = joined(tok_full[pl.ds(micro * (length // RUN) + s * 2, 2)]).astype(F32)
+        total = own + total
+        resid[micro] = total
+        root = lax.rsqrt(row_mean(total * total) + EPSILON)
+        post_own[micro] = (total * root * gains[1:2]).astype(BF16)
+        to = post_full.at[micro, mine]
+        posts.append((wire.send(post_own.at[micro], to, p.x_dev), wire.send(post_own.at[micro], to, p.core_dev),
+                      wire.own(post_own.at[micro], to)))
+    for micro in range(2):
+        posts[micro][0].wait_recv()
+        block = post_full.at[micro, theirs]
+        wire.send(block, block, p.core_dev).wait_recv()
+        posts[micro][1].wait_recv()
+        posts[micro][2].wait()
+    for copy in back_core:
+        copy.wait_recv()
+    for copy in back_kept:
+        copy.wait()
+    for state in wide_states + [down_state]:
+        settle(state)
+    down_kept.wait()
+    reducer.close()
+    wire.close()
+
+
+def front(planes, order, rank, tokens, cotangent, gain_tile, cosine, sine, shards):
+    nf = 2 * planes
+    rows = tokens.shape[1]
+    length = 4 * rows
+    total = 2 * length
+    tokens = tokens.reshape(2, 2, RUN, tokens.shape[2])
+    quarter = [item.shape[1] // 4 for item in shards[:3]] + [None] + [item.shape[1] // 4 for item in shards[4:6]]
+    def col(at):
+        return jax.ShapeDtypeStruct((4, nf, shards[at].shape[0], quarter[at]), BF16)
+    def row(at):
+        return jax.ShapeDtypeStruct((nf, *shards[at].shape), BF16)
+    def low(width):
+        return jax.ShapeDtypeStruct((total, width), BF16)
+    shapes = [col(0), col(1), col(2), row(3), col(4), col(5), row(6),
+              low(1024), low(512), low(256), low(256), low(512), low(256),
+              jax.ShapeDtypeStruct((total, 8), F32),
+              jax.ShapeDtypeStruct((total // RUN, RUN, 512), BF16), jax.ShapeDtypeStruct((4, length, 2), F32),
+              jax.ShapeDtypeStruct((2, rows, 1024), F32),
+              jax.ShapeDtypeStruct((2, length, 1024), BF16), jax.ShapeDtypeStruct((2, length, 1024), BF16),
+              jax.ShapeDtypeStruct((8, 1024), F32)]
+    far = {4, 5, 6, 17, 18}
+    vm = pl.BlockSpec(memory_space=VMEM)
+    hb = pl.BlockSpec(memory_space=ANY)
+    sm = pl.BlockSpec(memory_space=pltpu.SMEM)
+    return pl.pallas_call(
+        functools.partial(front_kernel, planes),
+        out_shape=shapes,
+        in_specs=[sm, sm, hb, hb, vm, vm, vm] + [hb] * 7,
+        out_specs=[hb if at in far else vm for at in range(len(shapes))],
+        scratch_shapes=[
+            VMEM((total // RUN, RUN, 1024), BF16), VMEM((4, nf, 8, RUN), F32), VMEM((2, rows, 1024), BF16),
+            VMEM((BLOCK, 1024), F32), *reducer_scratch(1024), *wire_scratch(120, 24),
+        ],
+        compiler_params=pltpu.CompilerParams(
+            collective_id=0, has_side_effects=True, vmem_limit_bytes=VMEM_BYTES),
+        name="front",
+    )(order, rank, tokens, cotangent, gain_tile, cosine, sine, *shards)
+
+
+def middle_kernel(
+    planes,
+    post, back, wg, wu, wd, resid, gains,
+    grad_g, grad_u, grad_d, y_out, y_keep, d_resid, attn_full, sums,
+    hidden, d_gate, d_up, part_y, part_p, attn_own,
+    y_core_out, y_core_in,
+    core_out, core_in, x_out, x_in, keep, core_s, core_r, x_s, x_r,
+    y_core_s, y_core_r, out_sems, in_sems, own_sems,
+):
+    p = Place(planes)
+    s = p.s
+    wire = Wire(out_sems, in_sems, own_sems)
+    into_post = Reducer(p, part_p, core_out, core_in, x_out, x_in, keep, (core_s, core_r, x_s, x_r))
+    into_out = Reducer(p, part_y, y_core_out, y_core_in, y_out, None, y_keep, (y_core_s, y_core_r, None, None))
+    rows = resid.shape[1]
+    length = 4 * rows
+    mine = pl.ds(s * rows, rows)
+    theirs = pl.ds(p.x_dev[0] * rows, rows)
+    p.meet()
+
+    def feed(step, carry):
+        micro, block = into_post.block(step)
+        here = pl.ds(pl.multiple_of(micro * length + block * BLOCK, BLOCK), BLOCK)
+        given, pulled = post[here, :], back[here, :]
+        gate = dot(given, wg[...])
+        upper = dot(given, wu[...])
+        d_hidden = dot(pulled, wd[...], NARROW)
+        sigma = 1.0 / (1.0 + jnp.exp(-gate))
+        lit = gate * sigma
+        low = (lit * upper).astype(BF16)
+        gate_low = (d_hidden * upper * sigma * (1.0 + gate * (1.0 - sigma))).astype(BF16)
+        up_low = (d_hidden * lit).astype(BF16)
+        hidden[here] = low
+        d_gate[here] = gate_low
+        d_up[here] = up_low
+        part_p[...] = dot(gate_low, wg[...], NARROW) + dot(up_low, wu[...], NARROW)
+        into_post.take(step)
+        part_y[...] = dot(low, wd[...])
+        into_out.take(step, send_x=False)
+        return carry
+
+    lax.fori_loop(0, 8, feed, 0)
+
+    def down_tile(at, carry):
+        cut = pl.ds(pl.multiple_of(at * BLOCK, BLOCK), BLOCK)
+        grad_d[cut] = dot(hidden[:, cut], back[...], TALL).astype(BF16)
+        return carry
+
+    def gate_tile(at, carry):
+        cut = pl.ds(pl.multiple_of(at * BLOCK, BLOCK), BLOCK)
+        grad_g[cut] = dot(post[:, cut], d_gate[...], TALL).astype(BF16)
+        return carry
+
+    def up_tile(at, carry):
+        cut = pl.ds(pl.multiple_of(at * BLOCK, BLOCK), BLOCK)
+        grad_u[cut] = dot(post[:, cut], d_up[...], TALL).astype(BF16)
+        return carry
+
+    gain = gains[1:2]
+    sends = []
+    sums[...] = jnp.zeros_like(sums)
+
+    def settle(micro):
+        grad = into_post.total(micro)
+        held = resid[micro]
+        root = lax.rsqrt(row_mean(held * held) + EPSILON)
+        unit = held * root
+        sums[0:1] += jnp.sum(grad * unit, axis=0, keepdims=True)
+        scaled = grad * gain
+        own = back[pl.ds(pl.multiple_of(micro * length + s * rows, rows), rows), :].astype(F32)
+        whole = own + root * (scaled - unit * row_mean(scaled * unit))
+        d_resid[micro] = whole
+        attn_own[micro] = whole.astype(BF16)
+        to = attn_full.at[micro, mine]
+        sends.append((wire.send(attn_own.at[micro], to, p.x_dev), wire.send(attn_own.at[micro], to, p.core_dev),
+                      wire.own(attn_own.at[micro], to)))
+        y_keep[micro] = y_keep[micro] + held
+
+    lax.fori_loop(0, 3, down_tile, 0)
+    settle(0)
+    lax.fori_loop(0, 4, gate_tile, 0)
+    settle(1)
+    lax.fori_loop(0, 4, up_tile, 0)
+    for micro in range(2):
+        sends[micro][0].wait_recv()
+        block = attn_full.at[micro, theirs]
+        wire.send(block, block, p.core_dev).wait_recv()
+        sends[micro][1].wait_recv()
+        sends[micro][2].wait()
+    into_post.close()
+    into_out.close(send_x=False)
+    wire.close()
+
+
+def middle(planes, post, back, wg, wu, wd, resid, gains):
+    rows = resid.shape[1]
+    total = 8 * rows
+    wide = wg.shape[1]
+    shapes = [
+        jax.ShapeDtypeStruct((1024, wide), BF16), jax.ShapeDtypeStruct((1024, wide), BF16),
+        jax.ShapeDtypeStruct((wide, 1024), BF16),
+        jax.ShapeDtypeStruct((2, rows, 1024), BF16), jax.ShapeDtypeStruct((2, rows, 1024), F32),
+        jax.ShapeDtypeStruct((2, rows, 1024), F32), jax.ShapeDtypeStruct((2, 4 * rows, 1024), BF16),
+        jax.ShapeDtypeStruct((8, 1024), F32),
+    ]
+    vm = pl.BlockSpec(memory_space=VMEM)
+    hb = pl.BlockSpec(memory_space=ANY)
+    return pl.pallas_call(
+        functools.partial(middle_kernel, planes),
+        out_shape=shapes,
+        in_specs=[vm] * 7,
+        out_specs=[vm] * 6 + [hb, vm],
+        scratch_shapes=[
+            VMEM((total, wide), BF16), VMEM((total, wide), BF16), VMEM((total, wide), BF16),
+            VMEM((BLOCK, 1024), F32), VMEM((BLOCK, 1024), F32), VMEM((2, rows, 1024), BF16),
+            VMEM((4, BLOCK, 1024), BF16), VMEM((4, BLOCK, 1024), BF16),
+            *reducer_scratch(1024),
+            pltpu.SemaphoreType.DMA((4,)), pltpu.SemaphoreType.DMA((4,)),
+            *wire_scratch(8, 4),
+        ],
+        compiler_params=pltpu.CompilerParams(
+            collective_id=1, has_side_effects=True, vmem_limit_bytes=VMEM_BYTES),
+        name="middle",
+    )(post, back, wg, wu, wd, resid, gains)
+
+
+class Homing:
+    def __init__(self, place, wire, grad, came, sums, far, turned, home):
+        self.p, self.wire, self.grad, self.came, self.sums = place, wire, grad, came, sums
+        self.far, self.turned, self.home = far, turned, home
+        self.by_columns = len(grad.shape) == 5
+
+    def side(self, ref, y):
+        return ref.at[:, :, y] if self.by_columns else ref.at[:, y]
+
+    def start(self):
+        self.kept = self.wire.own(self.side(self.grad, self.p.y), self.sums)
+        self.sent = self.wire.send(self.side(self.grad, self.p.other_y), self.came, self.p.y_dev)
+
+    def plane(self, ref, z):
+        return ref.at[:, z] if self.by_columns else ref.at[z]
+
+    def spread(self):
+        self.kept.wait()
+        self.sent.wait_recv()
+
+        def add(z, carry):
+            at = (slice(None), z) if self.by_columns else (z,)
+            self.sums[at] = (self.sums[at].astype(F32) + self.came[at].astype(F32)).astype(BF16)
+            return carry
+
+        lax.fori_loop(0, self.p.planes, add, 0)
+        self.out = [
+            self.wire.send(self.plane(self.sums, self.p.z_at(step)), self.far.at[step - 1], self.p.z_dev(step))
+            for step in range(1, self.p.planes)
+        ]
+
+    def gather(self):
+        for copy in self.out:
+            copy.wait_recv()
+        at = (slice(None), self.p.z) if self.by_columns else (self.p.z,)
+        total = self.sums[at].astype(F32)
+        for step in range(1, self.p.planes):
+            total = total + self.far[step - 1].astype(F32)
+        if not self.by_columns:
+            self.home[...] = total
+            return
+        leave, arrive, own = self.turned
+        s = self.p.s
+        leave[...] = total.astype(BF16)
+        own[...] = total
+        self.back = []
+        for dev in (self.p.core_dev, self.p.x_dev, self.p.far_dev):
+            self.back.append((dev[0], self.wire.send(leave.at[dev[0]], arrive.at[s], dev)))
+
+    def finish(self):
+        if not self.by_columns:
+            return
+        leave, arrive, own = self.turned
+        width = own.shape[-1]
+        s = self.p.s
+        self.home[:, pl.ds(pl.multiple_of(s * width, RUN), width)] = own[s]
+        for owner, copy in self.back:
+            copy.wait_recv()
+            self.home[:, pl.ds(pl.multiple_of(owner * width, RUN), width)] = arrive[owner].astype(F32)
+
+
+def homing_scratch(planes, shape):
+    kept = shape[:-3] + shape[-2:]
+    once = shape[:-4] + shape[-2:]
+    found = [VMEM(kept, BF16), VMEM(kept, BF16), VMEM((planes - 1, *once), BF16)]
+    if len(shape) == 5:
+        found += [VMEM(once, BF16), VMEM(once, BF16), VMEM(once, F32)]
+    return found
+
+
+def homing_of(place, wire, grad, home, refs):
+    refs = list(refs)
+    count = 6 if len(grad.shape) == 5 else 3
+    mine, rest = refs[:count], refs[count:]
+    return Homing(place, wire, grad, *mine[:3], mine[3:], home), rest
+
+
+def turn_kernel(
+    planes,
+    order, attn, query, key, value, q_unit, k_unit, roots, mixed, lse, wo, cosine, sine, gains,
+    y_out, y_keep, sums_in, grad_g, grad_u, grad_d,
+    d_q, d_k, d_v, grad_o, sums, block_out, home_g, home_u, home_d,
+    d_mixed, attn_sorted, keys_grad, values_grad, y_in, *rest,
+):
+    p = Place(planes)
+    wire = Wire(*rest[-3:])
+    refs = list(rest[:-3])
+    rows = y_keep.shape[1]
+    length = 4 * rows
+    p.meet()
+    homes = []
+    for grad, home in ((grad_d, home_d), (grad_g, home_g), (grad_u, home_u)):
+        one, refs = homing_of(p, wire, grad, home, refs)
+        one.start()
+        homes.append(one)
+    y_sent = [wire.send(y_out.at[micro], y_in.at[micro], p.x_dev) for micro in range(2)]
+
+    def draw(step, carry):
+        here = pl.ds(pl.multiple_of(step * BLOCK, BLOCK), BLOCK)
+        low = two_runs(attn, order[step * 2], order[step * 2 + 1])
+        attn_sorted[here] = low
+        d_mixed[here] = dot(low, wo[...], NARROW).astype(BF16)
+        return carry
+
+    lax.fori_loop(0, 2 * length // BLOCK, draw, 0)
+
+    def out_tile(at, carry):
+        cut = pl.ds(pl.multiple_of(at * BLOCK, BLOCK), BLOCK)
+        grad_o[cut] = dot(mixed[:, cut], attn_sorted[...], TALL).astype(BF16)
+        return carry
+
+    lax.fori_loop(0, 2, out_tile, 0)
+    sums[...] = sums_in[...]
+
+    def lane_of(ref, here, lane):
+        held = ref[here, :]
+        lanes = lax.broadcasted_iota(jnp.int32, held.shape, 1)
+        return jnp.sum(jnp.where(lanes == lane, held, 0.0), axis=1, keepdims=True)
+
+    def norm_home(grad, cos, sin, unit, root, gain):
+        turned = grad * cos - pltpu.roll(grad, HEAD_DIM // 2, 1) * sin
+        scaled = turned * gain
+        back = root * (scaled - unit * row_mean(scaled * unit))
+        return back, jnp.sum(turned * unit, axis=0, keepdims=True)
+
+    def attend_back(step, carry):
+        micro, head = step // 2, lax.rem(step, 2)
+        keys_at = pl.ds(pl.multiple_of(head * HEAD_DIM, HEAD_DIM), HEAD_DIM)
+        lanes = [pl.ds(pl.multiple_of(head * 2 * HEAD_DIM + g * HEAD_DIM, HEAD_DIM), HEAD_DIM) for g in range(2)]
+        q_gain, k_gain = gains[2:3, 0:RUN], gains[3:4, 0:RUN]
+        keys_grad[...] = jnp.zeros_like(keys_grad)
+        values_grad[...] = jnp.zeros_like(values_grad)
+        for block in range(length // BLOCK):
+            here = pl.ds(pl.multiple_of(micro * length + block * BLOCK, BLOCK), BLOCK)
+            seen = (block + 1) * BLOCK
+            past = pl.ds(pl.multiple_of(micro * length, BLOCK), seen)
+            asked = jnp.concatenate([query[here, lane] for lane in lanes], axis=0)
+            pulled = jnp.concatenate([d_mixed[here, lane] for lane in lanes], axis=0)
+            given = jnp.concatenate([mixed[here, lane] for lane in lanes], axis=0)
+            level = jnp.concatenate(
+                [lse[step, pl.ds(block * BLOCK, BLOCK), g : g + 1] for g in range(2)], axis=0)
+            delta = jnp.sum(pulled.astype(F32) * given.astype(F32), axis=1, keepdims=True)
+            scores = dot(asked, key[past, keys_at], NARROW)
+            line = lax.broadcasted_iota(jnp.int32, (2 * BLOCK, seen), 0)
+            line = jnp.where(line >= BLOCK, line - BLOCK, line) + block * BLOCK
+            column = lax.broadcasted_iota(jnp.int32, (2 * BLOCK, seen), 1)
+            weight = jnp.exp2(scores * (SCALE * LOG2E) - level)
+            weight = jnp.where(column <= line, weight, 0.0)
+            d_soft = dot(pulled, value[past, keys_at], NARROW)
+            d_scores = (weight * (d_soft - delta)).astype(BF16)
+            values_grad[0:seen] += dot(weight.astype(BF16), pulled, TALL)
+            keys_grad[0:seen] += dot(d_scores, asked, TALL)
+            moved = dot(d_scores, key[past, keys_at]) * SCALE
+            spin = slice(block * BLOCK, (block + 1) * BLOCK)
+            for g, lane in enumerate(lanes):
+                root = lane_of(roots, here, head * 2 + g)
+                unit = q_unit[here, lane].astype(F32)
+                back, gained = norm_home(
+                    moved[g * BLOCK : (g + 1) * BLOCK], cosine[spin], sine[spin], unit, root, q_gain)
+                d_q[here, lane] = back.astype(BF16)
+                sums[1:2, 0:RUN] += gained
+        everything = pl.ds(pl.multiple_of(micro * length, BLOCK), length)
+        root = lane_of(roots, everything, head + 4)
+        unit = k_unit[everything, keys_at].astype(F32)
+        back, gained = norm_home(keys_grad[...] * SCALE, cosine[...], sine[...], unit, root, k_gain)
+        d_k[everything, keys_at] = back.astype(BF16)
+        sums[2:3, 0:RUN] += gained
+        d_v[everything, keys_at] = values_grad[...].astype(BF16)
+        return carry
+
+    lax.fori_loop(0, 1, attend_back, 0)
+    homes[0].spread()
+    lax.fori_loop(1, 2, attend_back, 0)
+    homes[1].spread()
+    for micro in range(2):
+        y_sent[micro].wait_recv()
+        block_out[micro] = (y_keep[micro] + y_in[micro].astype(F32)).astype(BF16)
+    lax.fori_loop(2, 4, attend_back, 0)
+    homes[2].spread()
+    for one in homes:
+        one.gather()
+    for one in homes:
+        one.finish()
+    wire.close()
+
+
+def turn(planes, order, attn, query, key, value, q_unit, k_unit, roots, mixed, lse, wo, cosine, sine, gains,
+         y_out, y_keep, sums, grad_g, grad_u, grad_d):
+    rows = y_keep.shape[1]
+    length = 4 * rows
+    total = 2 * length
+    shapes = [
+        jax.ShapeDtypeStruct((total, 512), BF16), jax.ShapeDtypeStruct((total, 256), BF16),
+        jax.ShapeDtypeStruct((total, 256), BF16), jax.ShapeDtypeStruct((512, 1024), BF16),
+        jax.ShapeDtypeStruct((8, 1024), F32), jax.ShapeDtypeStruct((2, rows, 1024), BF16),
+        jax.ShapeDtypeStruct((grad_g.shape[3], 4 * grad_g.shape[4]), F32),
+        jax.ShapeDtypeStruct((grad_u.shape[3], 4 * grad_u.shape[4]), F32),
+        jax.ShapeDtypeStruct(grad_d.shape[2:], F32),
+    ]
+    vm = pl.BlockSpec(memory_space=VMEM)
+    hb = pl.BlockSpec(memory_space=ANY)
+    sm = pl.BlockSpec(memory_space=pltpu.SMEM)
+    return pl.pallas_call(
+        functools.partial(turn_kernel, planes),
+        out_shape=shapes,
+        in_specs=[sm] + [vm] * 13 + [hb, vm, vm] + [hb] * 3,
+        out_specs=[vm] * len(shapes),
+        scratch_shapes=[
+            VMEM((total, 512), BF16), VMEM((total, 1024), BF16), VMEM((length, HEAD_DIM), F32),
+            VMEM((length, HEAD_DIM), F32), VMEM((2, rows, 1024), BF16),
+            *homing_scratch(planes, grad_d.shape), *homing_scratch(planes, grad_g.shape),
+            *homing_scratch(planes, grad_u.shape), *wire_scratch(24, 4),
+        ],
+        compiler_params=pltpu.CompilerParams(
+            collective_id=2, has_side_effects=True, vmem_limit_bytes=VMEM_BYTES),
+        name="turn",
+    )(order, attn, query, key, value, q_unit, k_unit, roots, mixed, lse, wo, cosine, sine, gains,
+      y_out, y_keep, sums, grad_g, grad_u, grad_d)
+
+
+def last_kernel(
+    planes,
+    rank, normed, d_q, d_k, d_v, wq, wk, wv, tokens, d_resid, gains, sums_in, grad_o,
+    token_grad, sums, home_q, home_k, home_v, home_o,
+    grad_q, grad_k, grad_v, part, sums_out, sums_came,
+    core_out, core_in, x_out, x_in, keep, core_s, core_r, x_s, x_r, *rest,
+):
+    p = Place(planes)
+    s, f = p.s, p.f
+    wire = Wire(*rest[-3:])
+    refs = list(rest[:-3])
+    reducer = Reducer(p, part, core_out, core_in, x_out, x_in, keep, (core_s, core_r, x_s, x_r))
+    rows = tokens.shape[1]
+    length = 4 * rows
+    p.meet()
+    out_home, refs = homing_of(p, wire, grad_o, home_o, refs)
+    out_home.start()
+    homes = []
+    for grad, pulled, home in ((grad_q, d_q, home_q), (grad_k, d_k, home_k), (grad_v, d_v, home_v)):
+        def tile(at, carry, grad=grad, pulled=pulled):
+            cut = pl.ds(pl.multiple_of(at * BLOCK, BLOCK), BLOCK)
+            found = dot(joined(normed[:, :, cut]), flat(pulled), TALL).astype(BF16)
+            grad[at] = found.reshape(grad.shape[1:])
+            return carry
+
+        lax.fori_loop(0, 4, tile, 0)
+        one, refs = homing_of(p, wire, grad, home, refs)
+        one.start()
+        homes.append(one)
+    sums[...] = sums_in[...]
+
+    def pull(step, carry):
+        micro, block = reducer.block(step)
+        at = micro * (length // RUN) + block * 2
+        runs = (rank[at], rank[at + 1])
+        found = dot(two_runs(d_q, *runs), wq[...], NARROW)
+        found += dot(two_runs(d_k, *runs), wk[...], NARROW)
+        found += dot(two_runs(d_v, *runs), wv[...], NARROW)
+        part[...] = found
+        sums[3:4] += jnp.sum(found * two_runs(normed, *runs).astype(F32), axis=0, keepdims=True)
+        reducer.take(step)
+        return carry
+
+    lax.fori_loop(0, 8, pull, 0)
+    out_home.spread()
+    sums[3:4] = sums[3:4] / gains[0:1]
+
+    def exchange(stage, devices, base):
+        sums_out[stage] = sums[...]
+        sent = [wire.send(sums_out.at[stage], sums_came.at[base + at], dev) for at, dev in enumerate(devices)]
+        return base, sent
+
+    def absorb(state):
+        base, sent = state
+        total = sums[...]
+        for at, copy in enumerate(sent):
+            copy.wait_recv()
+            total = total + sums_came[base + at]
+        sums[...] = total
+
+    state = exchange(0, (p.core_dev, p.x_dev, p.far_dev), 0)
+    for one in homes:
+        one.spread()
+    absorb(state)
+    state = exchange(1, [p.z_dev(step) for step in range(1, planes)], 3)
+    out_home.gather()
+    absorb(state)
+    state = exchange(2, [p.y_dev], 2 + planes)
+    for micro in range(2):
+        grad = reducer.total(micro)
+        held = tokens[micro].astype(F32)
+        root = lax.rsqrt(row_mean(held * held) + EPSILON)
+        unit = held * root
+        scaled = grad * gains[0:1]
+        token_grad[micro] = d_resid[micro] + root * (scaled - unit * row_mean(scaled * unit))
+    for one in homes:
+        one.gather()
+    absorb(state)
+    for one in homes:
+        one.finish()
+    reducer.close()
+    wire.close()
+
+
+def last(planes, rank, normed, d_q, d_k, d_v, wq, wk, wv, tokens, d_resid, gains, sums, grad_o):
+    nf = 2 * planes
+    rows = tokens.shape[1]
+    widths = [wq.shape[1], wk.shape[1], wv.shape[1]]
+    deep = 1024 // (4 * nf)
+    grads = [(4, planes, 2, deep, wide) for wide in widths]
+    shapes = [
+        jax.ShapeDtypeStruct((2, rows, 1024), F32), jax.ShapeDtypeStruct((8, 1024), F32),
+        *[jax.ShapeDtypeStruct((deep, 4 * wide), F32) for wide in widths],
+        jax.ShapeDtypeStruct(grad_o.shape[2:], F32),
+    ]
+    vm = pl.BlockSpec(memory_space=VMEM)
+    hb = pl.BlockSpec(memory_space=ANY)
+    sm = pl.BlockSpec(memory_space=pltpu.SMEM)
+    scratch = [VMEM(shape, BF16) for shape in grads]
+    scratch += [VMEM((BLOCK, 1024), F32), VMEM((3, 8, 1024), F32), VMEM((3 + planes, 8, 1024), F32)]
+    scratch += [*reducer_scratch(1024), *homing_scratch(planes, grad_o.shape)]
+    for shape in grads:
+        scratch += homing_scratch(planes, shape)
+    return pl.pallas_call(
+        functools.partial(last_kernel, planes),
+        out_shape=shapes,
+        in_specs=[sm] + [vm] * 11 + [hb],
+        out_specs=[vm] * len(shapes),
+        scratch_shapes=scratch + wire_scratch(48, 4),
+        compiler_params=pltpu.CompilerParams(
+            collective_id=3, has_side_effects=True, vmem_limit_bytes=VMEM_BYTES),
+        name="last",
+    )(rank, normed, d_q, d_k, d_v, wq, wk, wv, tokens, d_resid, gains, sums, grad_o)
+
+
+def run_tables(positions):
+    runs = positions.shape[1] // RUN
+    rank = positions[:, ::RUN] // RUN
+    index = jnp.arange(runs, dtype=jnp.int32)
+    order = jnp.sum(jnp.where(rank[:, :, None] == index, index[None, :, None], 0), axis=1)
+    base = jnp.arange(positions.shape[0], dtype=jnp.int32)[:, None] * runs
+    return (order + base).reshape(-1), (rank + base).reshape(-1)
+
+
+def kernel_body(tokens, positions, g_in, g_post, g_query, g_key, w_query, w_key, w_value,
+                w_out, w_gate, w_up, w_down, cotangent):
+    planes = lax.axis_size("fsdp") // 2
+    length = positions.shape[2]
+    order, rank = run_tables(positions[:, 0])
+    tile = jnp.stack(
+        [jnp.pad(item.astype(F32), (0, RUN - item.shape[0])) for item in (g_in, g_post, g_query, g_key)])
+    tile = jnp.pad(tile, ((0, 4), (0, 0)))
+    cosine, sine = rope_tables(jnp.arange(length))
+    cosine, sine = cosine[:, 0], sine[:, 0]
+    half = HEAD_DIM // 2
+    sine = jnp.concatenate([-sine[:, :half], sine[:, half:]], axis=1)
+    near = tokens[:, 0]
+    shards = (w_query, w_key, w_value, w_out, w_gate, w_up, w_down)
+    (wq, wk, wv, wo, wg, wu, wd, normed, query, key, value, q_unit, k_unit, roots, mixed, lse,
+     resid, post, back, gains) = front(
+        planes, order, rank, near, cotangent[:, 0], tile, cosine, sine, shards)
+    wq, wk, wv, wo, wg, wu, wd = [
+        item.reshape(-1, item.shape[-1]) for item in (wq, wk, wv, wo, wg, wu, wd)]
+    post, back = post.reshape(-1, post.shape[-1]), back.reshape(-1, back.shape[-1])
+    grad_g, grad_u, grad_d, y_out, y_keep, d_resid, attn, sums = middle(
+        planes, post, back, wg, wu, wd, resid, gains)
+    apart = lambda item: item.reshape(-1, RUN, item.shape[-1])
+    columns = lambda item: item.reshape(4, planes, 2, -1, item.shape[-1])
+    lines = lambda item: item.reshape(planes, 2, -1, item.shape[-1])
+    d_q, d_k, d_v, grad_o, sums, block_out, home_g, home_u, home_d = turn(
+        planes, order, apart(attn), query, key, value, q_unit, k_unit, roots,
+        mixed.reshape(-1, mixed.shape[-1]), lse,
+        wo, cosine, sine, gains, y_out, y_keep, sums, columns(grad_g), columns(grad_u), lines(grad_d))
+    token_grad, sums, home_q, home_k, home_v, home_o = last(
+        planes, rank, apart(normed), apart(d_q), apart(d_k), apart(d_v), wq, wk, wv, near, d_resid, gains, sums, lines(grad_o))
+    me = lax.axis_index("seq") * (2 * planes) + lax.axis_index("fsdp")
+    small = [
+        lax.dynamic_slice(sums, (row, me * item.shape[0]), (1, item.shape[0]))[0]
+        for row, item in ((3, g_in), (0, g_post), (1, g_query), (2, g_key))
+    ]
+    return (block_out[:, None], token_grad[:, None], *small, home_q, home_k, home_v, home_o,
+            home_g, home_u, home_d)
+
+
 def solution(mesh):
     both = ("seq", "fsdp")
     act = P(None, "fsdp", "seq", None)
     vec, mat = P(both), P(both, None)
+
+    def body(*args):
+        rows = args[6].shape[0]
+        fits = mesh.shape["seq"] == 4 and mesh.shape["fsdp"] % 2 == 0 and rows % 16 == 0
+        return (kernel_body if fits else plain_body)(*args)
+
     return jax.shard_map(
-        plain_body,
+        body,
         mesh=mesh,
         in_specs=(act, P(None, "fsdp", None), *[vec] * 4, *[mat] * 7, act),
         out_specs=(act, act, *[vec] * 4, *[mat] * 7),

time: 1190 us -> 421 us (0.35)
  waiting for transfers between devices: 713 us -> 0 us
  Pallas kernels: 0 us -> 401 us
  matrix products: 210 us -> 0 us
  blocking collectives: 100 us -> 0 us
  other arithmetic: 88.3 us -> 4.06 us
  local copies, waits for them, and re-layouts: 36.5 us -> 11.4 us
  starting transfers between devices: 19.6 us -> 0 us
  between operations: 16.6 us -> 1.01 us
    reduce_scatter x15 -> x0, waiting for transfers between devices: 499 us -> none  [the longest x10 258 us: sum_scatter(): lax.psum_scatter(part.astype(BF16), axis, scatter_dimension=0, tiled=True)]
    pallas_call x0 -> x4, Pallas kernels: none -> 401 us  [the longest x1 165 us: front(): pl.pallas_call(functools.partial(front_kernel, planes), out_shape=shapes,...]
    all_gather x12 -> x0, waiting for transfers between devices: 201 us -> none  [the longest x8 108 us: gather_rows(): return lax.all_gather(item, 'seq', axis=0, tiled=True)]
    dot_general x52 -> x0, matrix products: 186 us -> none  [mul(): return jnp.einsum(eq, left, right, preferred_element_type=F32)]
    unnamed x2 -> x0, blocking collectives: 80.2 us -> none
    convert_element_type x14 -> x0, other arithmetic: 41.2 us -> none  [the longest x2 24.7 us: plain_body(): (soft * (d_soft - jnp.sum(d_soft * soft, axis=-1, keepdims=True))).astype...]
    sub x2 -> x0, matrix products: 23.6 us -> none  [plain_body(): soft = jax.nn.softmax(scores, axis=-1)]
    all_to_all x2 -> x0, blocking collectives: 19.9 us -> none  [spread(): packed = lax.all_to_all(packed, 'seq', 0, 0, tiled=True)]
  transfers between devices with their start and end apart: 32 -> 0, of which waited for: 24 -> 0; matrix products, arithmetic and copies ran while one was open for 25% -> 0% of each run, Pallas kernels for 0% -> 0%
where the time goes in v2:
time: 421 us; the launch traced here: 418 us
  Pallas kernels  401 us (95%)
  local copies, waits for them, and re-layouts  11.4 us (3%)
    pallas_call x1, Pallas kernels, front(): pl.pallas_call(functools.partial(front_kernel, planes), out_shape=shapes,...  165 us
    pallas_call x1, Pallas kernels, middle(): pl.pallas_call(functools.partial(middle_kernel, planes), out_shape=shapes...  83.2 us
    pallas_call x1, Pallas kernels, turn(): pl.pallas_call(functools.partial(turn_kernel, planes), out_shape=shapes,...  82.9 us
    pallas_call x1, Pallas kernels, last(): pl.pallas_call(functools.partial(last_kernel, planes), out_shape=shapes,...  70.2 us

profile of v2, /device:TPU:0, one launch (start us, length us, event | category | flops | bytes accessed | tf_op | source)
XLA Modules:
  0.0 417.8 jit_solution(17746393254039592576)
XLA Ops:
  0.7 0.0 copy-start.9
  0.7 0.0 copy-start.10
  0.7 0.0 copy-start.11
  0.7 0.0 copy-start.12
  0.7 0.0 copy-start.13
  0.7 1.9 fusion
  2.6 1.3 pad_maximum_fusion
  4.0 0.1 slice.3
  4.1 0.1 broadcast_add_fusion
  4.1 0.1 select_reduce_fusion
  4.2 0.1 broadcast_add_fusion.1
  4.3 0.6 add.44.order
  4.9 0.6 fusion.8.gain_tile
  5.5 0.6 reshape.106.rank
  6.1 165.0 %front.1 = (bf16[4,8,32,512]{3,2,1,0:T(8,128)(2,1)}, bf16[4,8,32,256]{3,2,1,0:T(8,128)(2,1)}, bf16[4,8,32,256]{3,2,1,0:T(8,128)(2,1)}, bf16[8,64,1024]{2,1,0:T(8...) custom-call(s32[16]{0:T(128)} %add.44.order, ...), custom_call_target="tpu_custom_call" | custom-call | tf_op jit(solution)/shard_map/front/pallas_call | solution.py:613
  171.1 83.2 %middle.1 = (bf16[1024,768]{1,0:T(8,128)(2,1)}, bf16[1024,768]{1,0:T(8,128)(2,1)}, bf16[768,1024]{1,0:T(8,128)(2,1)}, bf16[2,256,1024]{2,1,0:T(8,128)(2,1)}, f32...) custom-call(bf16[2048,1024]{1,0:T(8,128)(2,1)} %bitcast.51, ...), custom_call_target="tpu_custom_call" | custom-call | tf_op jit(solution)/shard_map/middle/pallas_call | solution.py:735
  254.4 82.9 %turn.1 = (bf16[2048,512]{1,0:T(8,128)(2,1)}, bf16[2048,256]{1,0:T(8,128)(2,1)}, bf16[2048,256]{1,0:T(8,128)(2,1)}, bf16[512,1024]{1,0:T(8,128)(2,1)}, f32[8,102...) custom-call(s32[16]{0:T(128)} %add.44.order, ...), custom_call_target="tpu_custom_call" | custom-call | tf_op jit(solution)/shard_map/turn/pallas_call | solution.py:956
  337.3 70.2 %last.1 = (f32[2,256,1024]{2,1,0:T(8,128)}, f32[8,1024]{1,0:T(8,128)}, f32[32,2048]{1,0:T(8,128)}, f32[32,1024]{1,0:T(8,128)}, f32[32,1024]{1,0:T(8,128)}, /*index=5*/f32[64,1024]{1,0:T(8,128)}) custom-call(s32[16]{0:T(128)} %reshape.106.rank, bf16[16,128,1024]{2,1,0:T(8,128)(2,1)} %bitcast.47, bf16[16,128,512]{2,1,0:T(8,128)(2,1)} %bitcast.55, ...), custom_call_target="tpu_custom_call" | custom-call | tf_op jit(solution)/shard_map/last/pallas_call | solution.py:1077
  407.5 1.4 dynamic-slice_bitcast_fusion.2
  409.0 1.3 dynamic-slice_bitcast_fusion
  410.3 0.0 copy-done.1
  410.3 1.0 copy.43
  411.3 0.0 copy-done
  411.3 0.0 copy-start.5
  411.3 1.3 copy.44
  412.6 0.7 copy.45
  413.3 0.7 copy.46
  414.0 0.7 copy.47
  414.6 0.7 copy.48
  415.4 0.7 copy.49
  416.1 0.7 copy.50
  416.8 0.7 copy.51
  (26 shorter events, 0.1 us)
Async XLA Ops:
  0.7 3.3 copy-start.9
  0.7 4.2 %copy-start.10 = (bf16[4]{0:T(256)(128)(2,1)S(1)}, bf16[4]{0:T(256)(128)(2,1)}, u32[]{:S(2)}) copy-start(bf16[4]{0:T(256)(128)(2,1)} %param.19) | copy-start | bytes 28
  0.7 4.2 %copy-start.11 = (bf16[4]{0:T(256)(128)(2,1)S(1)}, bf16[4]{0:T(256)(128)(2,1)}, u32[]{:S(2)}) copy-start(bf16[4]{0:T(256)(128)(2,1)} %param.18) | copy-start | bytes 28
  0.7 4.2 %copy-start.12 = (bf16[32]{0:T(256)(128)(2,1)S(1)}, bf16[32]{0:T(256)(128)(2,1)}, u32[]{:S(2)}) copy-start(bf16[32]{0:T(256)(128)(2,1)} %param.17) | copy-start | bytes 196
  0.7 4.2 %copy-start.13 = (bf16[32]{0:T(256)(128)(2,1)S(1)}, bf16[32]{0:T(256)(128)(2,1)}, u32[]{:S(2)}) copy-start(bf16[32]{0:T(256)(128)(2,1)} %param.16) | copy-start | bytes 196
  337.3 73.0 %copy-start.1 = (bf16[2,256,1024]{2,1,0:T(8,128)(2,1)S(1)}, bf16[2,256,1024]{2,1,0:T(8,128)(2,1)}, u32[]{:S(2)}) copy-start(bf16[2,256,1024]{2,1,0:T(8,128)(2,1)} %get-tuple-element.79) | copy-start | bytes 3145732
  407.5 3.7 copy-start
  411.3 1.4 copy-start.6
  411.3 2.1 copy-start.8
  411.3 2.7 copy-start.7
  411.3 3.4 copy-start.5
  411.3 4.1 copy-start.4
  412.6 3.5 copy-start.3
  412.6 4.2 %copy-start.2 = (f32[96,1024]{1,0:T(8,128)S(1)}, f32[96,1024]{1,0:T(8,128)}, u32[]{:S(2)}) copy-start(f32[96,1024]{1,0:T(8,128)} %get-tuple-element.165) | copy-start | bytes 1179652

commit v3 on v2

--- a/solution.py
+++ b/solution.py
@@ -189,7 +189,7 @@
 PLAIN = (((1,), (0,)), ((), ()))
 LOG2E = 1.4426950408889634
 SCALE = HEAD_DIM ** (-0.5)
-VMEM_BYTES = 60 * 2**20
+VMEM_BYTES = 63 * 2**20
 
 
 def dot(left, right, dims=PLAIN):
@@ -275,8 +275,8 @@
     def block(self, step):
         p = self.place
         turn = step % 4
-        x = jnp.where(turn % 2 == 0, 1 - p.x, p.x)
-        c = jnp.where(turn < 2, 1 - p.c, p.c)
+        x = jnp.where(turn < 2, 1 - p.x, p.x)
+        c = jnp.where(turn % 2 == 0, 1 - p.c, p.c)
         return step // 4, x * 2 + c
 
     def core_copy(self, slot):
@@ -290,13 +290,13 @@
     def take(self, step, send_x=True):
         micro, turn = step // 4, step % 4
 
-        @pl.when(turn < 2)
+        @pl.when(turn % 2 == 0)
         def _():
-            slot = micro * 2 + turn
+            slot = micro * 2 + turn // 2
             self.core_out[slot] = self.part[...].astype(BF16)
             self.core_copy(slot).start()
 
-        @pl.when(turn == 2)
+        @pl.when(turn == 1)
         def _():
             slot = micro * 2
             self.core_copy(slot).wait_recv()
@@ -367,9 +367,10 @@
     planes,
     order, rank, tokens, cotangent, gain_tile, cosine, sine,
     s_q, s_k, s_v, s_o, s_g, s_u, s_d,
-    wq, wk, wv, wo, wg, wu, wd,
-    normed, query, key, value, q_unit, k_unit, roots, mixed, lse,
-    resid, post_full, back_full, gains,
+    wq_out, wk_out, wv_out, wo_out, wg, wu, wd,
+    normed_out, query_out, key_out, value_out, q_unit_out, k_unit_out, roots_out, mixed_out, lse_out,
+    resid_out, post_full, back_full, gains,
+    wq, wk, wv, wo, normed, query, key, value, q_unit, k_unit, roots, mixed, lse, resid,
     tok_full, gain_all, post_own, part,
     core_out, core_in, x_out, x_in, keep, core_s, core_r, x_s, x_r,
     out_sems, in_sems, own_sems,
@@ -416,10 +417,10 @@
     def blocks(full, at):
         return full.at[:, at] if len(full.shape) == 4 else full.at[at]
 
-    def push_planes(full):
+    def push_planes(full, side=True):
         here = blocks(full, f)
         far = [wire.send(here, here, p.z_dev(step)) for step in range(1, planes)]
-        return far, [wire.send(here, here, p.y_dev)]
+        return far, [wire.send(here, here, p.y_dev)] if side else []
 
     def forward(full, state):
         far, side = state
@@ -432,10 +433,10 @@
         for copy in state[1]:
             copy.wait_recv()
 
-    def push_rows(item, full):
+    def push_rows(item, full, side=True):
         kept = wire.own(item, full.at[f])
         far = [wire.send(item, full.at[f], p.z_dev(step)) for step in range(1, planes)]
-        return kept, (far, [wire.send(item, full.at[f], p.y_dev)])
+        return kept, (far, [wire.send(item, full.at[f], p.y_dev)] if side else [])
 
     for copy in gain_in:
         copy.wait_recv()
@@ -445,25 +446,18 @@
         arrived(group)
         states.append(push_planes(full))
     forward(gain_all, gain_state)
-    out_kept, out_state = push_rows(s_o, wo)
+    for full, state in zip((wq, wk, wv), states):
+        forward(full, state)
     tok_fwd = []
     for micro in range(2):
         tok_x[micro].wait_recv()
         block = tok_full.at[pl.ds(micro * (length // RUN) + p.x_dev[0] * 2, 2)]
         tok_fwd.append(wire.send(block, block, p.core_dev))
-    for full, state in zip((wq, wk, wv), states):
-        forward(full, state)
-    back_x, back_core, back_kept = [], [], []
-    for micro in range(2):
-        to = back_full.at[micro, mine]
-        back_x.append(wire.send(cotangent.at[micro], to, p.x_dev))
-        back_kept.append(wire.own(cotangent.at[micro], to))
-        back_core.append(wire.send(cotangent.at[micro], to, p.core_dev))
+    out_kept, out_state = push_rows(s_o, wo, side=False)
     wide_states = []
     for group, full in zip(second, (wg, wu)):
         arrived(group)
-        wide_states.append(push_planes(full))
-    down_kept, down_state = push_rows(s_d, wd)
+        wide_states.append(push_planes(full, side=False))
     settle(gain_state)
     table = gain_all[...].reshape(devices * 8, RUN).astype(BF16)
     gain_first = spread_gain(table, 0, devices, 1024)
@@ -475,12 +469,23 @@
     gains[1:2] = gain_post
     gains[2:3, 0:RUN] = gain_query
     gains[3:4, 0:RUN] = gain_key
+    for state in states:
+        settle(state)
+    saved = [wire.own(here, there) for here, there in ((wq, wq_out), (wk, wk_out), (wv, wv_out))]
+    out_state[1].append(wire.send(s_o, wo.at[f], p.y_dev))
+    for full, state in zip((wg, wu), wide_states):
+        state[1].append(wire.send(blocks(full, f), blocks(full, f), p.y_dev))
+    down_kept, down_state = push_rows(s_d, wd)
+    back_x, back_core, back_kept = [], [], []
+    for micro in range(2):
+        to = back_full.at[micro, mine]
+        back_x.append(wire.send(cotangent.at[micro], to, p.x_dev))
+        back_kept.append(wire.own(cotangent.at[micro], to))
+        back_core.append(wire.send(cotangent.at[micro], to, p.core_dev))
     for copy in tok_here:
         copy.wait()
     for copy in tok_core + tok_fwd:
         copy.wait_recv()
-    for state in states:
-        settle(state)
 
     def project(step, carry):
         here = pl.ds(pl.multiple_of(step * BLOCK, BLOCK), BLOCK)
@@ -508,9 +513,12 @@
         value[here] = dot(low, flat(wv)).astype(BF16)
         return carry
 
-    lax.fori_loop(0, 2 * length // BLOCK, project, 0)
-    for full, state in zip((wg, wu), wide_states):
-        forward(full, state)
+    lax.fori_loop(0, length // BLOCK, project, 0)
+    forward(wo, out_state)
+    lax.fori_loop(length // BLOCK, 2 * length // BLOCK, project, 0)
+    saved += [wire.own(here, there) for here, there in (
+        (normed, normed_out), (query, query_out), (key, key_out), (value, value_out),
+        (q_unit, q_unit_out), (k_unit, k_unit_out), (roots, roots_out))]
 
     def attend(step, carry):
         micro, head = step // 2, lax.rem(step, 2)
@@ -538,17 +546,6 @@
                 lse[step, pl.ds(block * BLOCK, BLOCK), g : g + 1] = level[half]
         return carry
 
-    lax.fori_loop(0, 2, attend, 0)
-    forward(wo, out_state)
-    forward(wd, down_state)
-    lax.fori_loop(2, 4, attend, 0)
-    for micro in range(2):
-        back_x[micro].wait_recv()
-        block = back_full.at[micro, theirs]
-        back_core.append(wire.send(block, block, p.core_dev))
-    out_kept.wait()
-    settle(out_state)
-
     def mix_out(step, carry):
         micro, block = reducer.block(step)
         at = micro * (length // RUN) + block * 2
@@ -557,7 +554,19 @@
         reducer.take(step)
         return carry
 
-    lax.fori_loop(0, 8, mix_out, 0)
+    lax.fori_loop(0, 2, attend, 0)
+    out_kept.wait()
+    settle(out_state)
+    lax.fori_loop(0, 4, mix_out, 0)
+    forward(wg, wide_states[0])
+    lax.fori_loop(2, 4, attend, 0)
+    saved += [wire.own(mixed, mixed_out), wire.own(lse, lse_out), wire.own(wo, wo_out)]
+    lax.fori_loop(4, 8, mix_out, 0)
+    forward(wu, wide_states[1])
+    for micro in range(2):
+        back_x[micro].wait_recv()
+        block = back_full.at[micro, theirs]
+        back_core.append(wire.send(block, block, p.core_dev))
     posts = []
     for micro in range(2):
         total = reducer.total(micro)
@@ -569,6 +578,8 @@
         to = post_full.at[micro, mine]
         posts.append((wire.send(post_own.at[micro], to, p.x_dev), wire.send(post_own.at[micro], to, p.core_dev),
                       wire.own(post_own.at[micro], to)))
+        saved.append(wire.own(resid.at[micro], resid_out.at[micro]))
+    forward(wd, down_state)
     for micro in range(2):
         posts[micro][0].wait_recv()
         block = post_full.at[micro, theirs]
@@ -582,6 +593,8 @@
     for state in wide_states + [down_state]:
         settle(state)
     down_kept.wait()
+    for copy in saved:
+        copy.wait()
     reducer.close()
     wire.close()
 
@@ -606,18 +619,20 @@
               jax.ShapeDtypeStruct((2, rows, 1024), F32),
               jax.ShapeDtypeStruct((2, length, 1024), BF16), jax.ShapeDtypeStruct((2, length, 1024), BF16),
               jax.ShapeDtypeStruct((8, 1024), F32)]
-    far = {4, 5, 6, 17, 18}
+    near = {19}
+    held = [shapes[at] for at in (0, 1, 2, 3, 7, 8, 9, 10, 11, 12, 13, 14, 15, 16)]
     vm = pl.BlockSpec(memory_space=VMEM)
     hb = pl.BlockSpec(memory_space=ANY)
     sm = pl.BlockSpec(memory_space=pltpu.SMEM)
     return pl.pallas_call(
         functools.partial(front_kernel, planes),
         out_shape=shapes,
-        in_specs=[sm, sm, hb, hb, vm, vm, vm] + [hb] * 7,
-        out_specs=[hb if at in far else vm for at in range(len(shapes))],
+        in_specs=[sm, sm] + [vm] * 12,
+        out_specs=[vm if at in near else hb for at in range(len(shapes))],
         scratch_shapes=[
+            *[VMEM(item.shape, item.dtype) for item in held],
             VMEM((total // RUN, RUN, 1024), BF16), VMEM((4, nf, 8, RUN), F32), VMEM((2, rows, 1024), BF16),
-            VMEM((BLOCK, 1024), F32), *reducer_scratch(1024), *wire_scratch(120, 24),
+            VMEM((BLOCK, 1024), F32), *reducer_scratch(1024), *wire_scratch(120, 48),
         ],
         compiler_params=pltpu.CompilerParams(
             collective_id=0, has_side_effects=True, vmem_limit_bytes=VMEM_BYTES),
@@ -625,11 +640,94 @@
     )(order, rank, tokens, cotangent, gain_tile, cosine, sine, *shards)
 
 
+class Homing:
+    def __init__(self, place, wire, by_columns, came=None, sums=None, far=None, turned=None, home=None):
+        self.p, self.wire, self.by_columns = place, wire, by_columns
+        self.came, self.sums, self.far, self.turned, self.home = came, sums, far, turned, home
+
+    def side(self, ref, y):
+        return ref.at[:, :, y] if self.by_columns else ref.at[:, y]
+
+    def plane(self, ref, z):
+        return ref.at[:, z] if self.by_columns else ref.at[z]
+
+    def start(self, grad):
+        self.kept = self.wire.own(self.side(grad, self.p.y), self.sums)
+        self.sent = self.wire.send(self.side(grad, self.p.other_y), self.came, self.p.y_dev)
+
+    def add(self):
+        self.kept.wait()
+        self.sent.wait_recv()
+
+        def add(z, carry):
+            at = (slice(None), z) if self.by_columns else (z,)
+            self.sums[at] = (self.sums[at].astype(F32) + self.came[at].astype(F32)).astype(BF16)
+            return carry
+
+        lax.fori_loop(0, self.p.planes, add, 0)
+
+    def push(self):
+        self.out = [
+            self.wire.send(self.plane(self.sums, self.p.z_at(step)), self.far.at[step - 1], self.p.z_dev(step))
+            for step in range(1, self.p.planes)
+        ]
+
+    def gather(self):
+        for copy in self.out:
+            copy.wait_recv()
+        at = (slice(None), self.p.z) if self.by_columns else (self.p.z,)
+        total = self.sums[at].astype(F32)
+        for step in range(1, self.p.planes):
+            total = total + self.far[step - 1].astype(F32)
+        if not self.by_columns:
+            self.home[...] = total
+            return
+        leave, arrive, own = self.turned
+        s = self.p.s
+        leave[...] = total.astype(BF16)
+        own[...] = total
+        self.back = []
+        for dev in (self.p.core_dev, self.p.x_dev, self.p.far_dev):
+            self.back.append((dev[0], self.wire.send(leave.at[dev[0]], arrive.at[s], dev)))
+
+    def finish(self):
+        if not self.by_columns:
+            return
+        leave, arrive, own = self.turned
+        width = own.shape[-1]
+        s = self.p.s
+        self.home[:, pl.ds(pl.multiple_of(s * width, RUN), width)] = own[s]
+        for owner, copy in self.back:
+            copy.wait_recv()
+            self.home[:, pl.ds(pl.multiple_of(owner * width, RUN), width)] = arrive[owner].astype(F32)
+
+
+def kept_shape(shape):
+    return shape[:-3] + shape[-2:]
+
+
+def once_shape(shape):
+    return shape[:-4] + shape[-2:]
+
+
+def y_scratch(shape):
+    return [VMEM(kept_shape(shape), BF16), VMEM(kept_shape(shape), BF16)]
+
+
+def z_scratch(planes, shape):
+    once = once_shape(shape)
+    found = [VMEM((planes - 1, *once), BF16)]
+    if len(shape) == 5:
+        found += [VMEM(once, BF16), VMEM(once, BF16), VMEM(once, F32)]
+    return found
+
+
 def middle_kernel(
     planes,
-    post, back, wg, wu, wd, resid, gains,
-    grad_g, grad_u, grad_d, y_out, y_keep, d_resid, attn_full, sums,
-    hidden, d_gate, d_up, part_y, part_p, attn_own,
+    post_in, back_in, wg_in, wu_in, wd_in, resid_in, gains,
+    gate_sums, grad_u, d_sums, y_out, y_keep, d_resid, attn_full, sums,
+    post, back, wg, wu, wd, resid, load_sems,
+    grad_g, grad_d, g_came, d_came, hidden, d_gate, d_up, part_y, part_p, attn_own,
     y_core_out, y_core_in,
     core_out, core_in, x_out, x_in, keep, core_s, core_r, x_s, x_r,
     y_core_s, y_core_r, out_sems, in_sems, own_sems,
@@ -643,11 +741,26 @@
     length = 4 * rows
     mine = pl.ds(s * rows, rows)
     theirs = pl.ds(p.x_dev[0] * rows, rows)
+    loads = [wire.own(wg_in, wg), wire.own(wu_in, wu), wire.own(wd_in, wd), wire.own(resid_in, resid)]
+
+    def chunk(step):
+        micro, block = into_post.block(step)
+        here = pl.ds(pl.multiple_of(micro * length + block * BLOCK, BLOCK), BLOCK)
+        return [pltpu.make_async_copy(far.at[here], near.at[here], load_sems.at[at, step])
+                for at, (far, near) in enumerate(((post_in, post), (back_in, back)))]
+
+    for step in range(8):
+        for copy in chunk(step):
+            copy.start()
     p.meet()
+    for copy in loads:
+        copy.wait()
 
     def feed(step, carry):
         micro, block = into_post.block(step)
         here = pl.ds(pl.multiple_of(micro * length + block * BLOCK, BLOCK), BLOCK)
+        for copy in chunk(step):
+            copy.wait()
         given, pulled = post[here, :], back[here, :]
         gate = dot(given, wg[...])
         upper = dot(given, wu[...])
@@ -666,21 +779,24 @@
         into_out.take(step, send_x=False)
         return carry
 
-    lax.fori_loop(0, 8, feed, 0)
+    down = Homing(p, wire, False, d_came, d_sums)
+    gate_home = Homing(p, wire, True, g_came, gate_sums)
 
     def down_tile(at, carry):
-        cut = pl.ds(pl.multiple_of(at * BLOCK, BLOCK), BLOCK)
-        grad_d[cut] = dot(hidden[:, cut], back[...], TALL).astype(BF16)
+        tall = hidden.shape[1] // 2
+        cut = pl.ds(pl.multiple_of(at * tall, RUN), tall)
+        found = dot(hidden[:, cut], back[...], TALL).astype(BF16)
+        grad_d[pl.ds(at * (planes // 2), planes // 2)] = found.reshape(planes // 2, *grad_d.shape[1:])
         return carry
 
     def gate_tile(at, carry):
         cut = pl.ds(pl.multiple_of(at * BLOCK, BLOCK), BLOCK)
-        grad_g[cut] = dot(post[:, cut], d_gate[...], TALL).astype(BF16)
+        grad_g[at] = dot(post[:, cut], d_gate[...], TALL).astype(BF16).reshape(grad_g.shape[1:])
         return carry
 
     def up_tile(at, carry):
         cut = pl.ds(pl.multiple_of(at * BLOCK, BLOCK), BLOCK)
-        grad_u[cut] = dot(post[:, cut], d_up[...], TALL).astype(BF16)
+        grad_u[at] = dot(post[:, cut], d_up[...], TALL).astype(BF16).reshape(grad_u.shape[1:])
         return carry
 
     gain = gains[1:2]
@@ -703,15 +819,24 @@
                       wire.own(attn_own.at[micro], to)))
         y_keep[micro] = y_keep[micro] + held
 
-    lax.fori_loop(0, 3, down_tile, 0)
+    lax.fori_loop(0, 7, feed, 0)
     settle(0)
+    lax.fori_loop(7, 8, feed, 0)
+    lax.fori_loop(0, 2, down_tile, 0)
+    down.start(grad_d)
     lax.fori_loop(0, 4, gate_tile, 0)
+    gate_home.start(grad_g)
     settle(1)
     lax.fori_loop(0, 4, up_tile, 0)
+    down.add()
+    forwards = []
     for micro in range(2):
         sends[micro][0].wait_recv()
         block = attn_full.at[micro, theirs]
-        wire.send(block, block, p.core_dev).wait_recv()
+        forwards.append(wire.send(block, block, p.core_dev))
+    gate_home.add()
+    for micro in range(2):
+        forwards[micro].wait_recv()
         sends[micro][1].wait_recv()
         sends[micro][2].wait()
     into_post.close()
@@ -723,9 +848,11 @@
     rows = resid.shape[1]
     total = 8 * rows
     wide = wg.shape[1]
+    tall = (4, planes, 2, 1024 // (8 * planes), wide)
+    flat_shape = (planes, 2, wide // (2 * planes), 1024)
     shapes = [
-        jax.ShapeDtypeStruct((1024, wide), BF16), jax.ShapeDtypeStruct((1024, wide), BF16),
-        jax.ShapeDtypeStruct((wide, 1024), BF16),
+        jax.ShapeDtypeStruct(kept_shape(tall), BF16), jax.ShapeDtypeStruct(tall, BF16),
+        jax.ShapeDtypeStruct(kept_shape(flat_shape), BF16),
         jax.ShapeDtypeStruct((2, rows, 1024), BF16), jax.ShapeDtypeStruct((2, rows, 1024), F32),
         jax.ShapeDtypeStruct((2, rows, 1024), F32), jax.ShapeDtypeStruct((2, 4 * rows, 1024), BF16),
         jax.ShapeDtypeStruct((8, 1024), F32),
@@ -735,15 +862,19 @@
     return pl.pallas_call(
         functools.partial(middle_kernel, planes),
         out_shape=shapes,
-        in_specs=[vm] * 7,
+        in_specs=[hb] * 6 + [vm],
         out_specs=[vm] * 6 + [hb, vm],
         scratch_shapes=[
+            *[VMEM(item.shape, item.dtype) for item in (post, back, wg, wu, wd, resid)],
+            pltpu.SemaphoreType.DMA((2, 8)),
+            VMEM(tall, BF16), VMEM(flat_shape, BF16), VMEM(kept_shape(tall), BF16),
+            VMEM(kept_shape(flat_shape), BF16),
             VMEM((total, wide), BF16), VMEM((total, wide), BF16), VMEM((total, wide), BF16),
             VMEM((BLOCK, 1024), F32), VMEM((BLOCK, 1024), F32), VMEM((2, rows, 1024), BF16),
             VMEM((4, BLOCK, 1024), BF16), VMEM((4, BLOCK, 1024), BF16),
             *reducer_scratch(1024),
             pltpu.SemaphoreType.DMA((4,)), pltpu.SemaphoreType.DMA((4,)),
-            *wire_scratch(8, 4),
+            *wire_scratch(16, 10),
         ],
         compiler_params=pltpu.CompilerParams(
             collective_id=1, has_side_effects=True, vmem_limit_bytes=VMEM_BYTES),
@@ -751,101 +882,33 @@
     )(post, back, wg, wu, wd, resid, gains)
 
 
-class Homing:
-    def __init__(self, place, wire, grad, came, sums, far, turned, home):
-        self.p, self.wire, self.grad, self.came, self.sums = place, wire, grad, came, sums
-        self.far, self.turned, self.home = far, turned, home
-        self.by_columns = len(grad.shape) == 5
-
-    def side(self, ref, y):
-        return ref.at[:, :, y] if self.by_columns else ref.at[:, y]
-
-    def start(self):
-        self.kept = self.wire.own(self.side(self.grad, self.p.y), self.sums)
-        self.sent = self.wire.send(self.side(self.grad, self.p.other_y), self.came, self.p.y_dev)
-
-    def plane(self, ref, z):
-        return ref.at[:, z] if self.by_columns else ref.at[z]
-
-    def spread(self):
-        self.kept.wait()
-        self.sent.wait_recv()
-
-        def add(z, carry):
-            at = (slice(None), z) if self.by_columns else (z,)
-            self.sums[at] = (self.sums[at].astype(F32) + self.came[at].astype(F32)).astype(BF16)
-            return carry
-
-        lax.fori_loop(0, self.p.planes, add, 0)
-        self.out = [
-            self.wire.send(self.plane(self.sums, self.p.z_at(step)), self.far.at[step - 1], self.p.z_dev(step))
-            for step in range(1, self.p.planes)
-        ]
-
-    def gather(self):
-        for copy in self.out:
-            copy.wait_recv()
-        at = (slice(None), self.p.z) if self.by_columns else (self.p.z,)
-        total = self.sums[at].astype(F32)
-        for step in range(1, self.p.planes):
-            total = total + self.far[step - 1].astype(F32)
-        if not self.by_columns:
-            self.home[...] = total
-            return
-        leave, arrive, own = self.turned
-        s = self.p.s
-        leave[...] = total.astype(BF16)
-        own[...] = total
-        self.back = []
-        for dev in (self.p.core_dev, self.p.x_dev, self.p.far_dev):
-            self.back.append((dev[0], self.wire.send(leave.at[dev[0]], arrive.at[s], dev)))
-
-    def finish(self):
-        if not self.by_columns:
-            return
-        leave, arrive, own = self.turned
-        width = own.shape[-1]
-        s = self.p.s
-        self.home[:, pl.ds(pl.multiple_of(s * width, RUN), width)] = own[s]
-        for owner, copy in self.back:
-            copy.wait_recv()
-            self.home[:, pl.ds(pl.multiple_of(owner * width, RUN), width)] = arrive[owner].astype(F32)
-
-
-def homing_scratch(planes, shape):
-    kept = shape[:-3] + shape[-2:]
-    once = shape[:-4] + shape[-2:]
-    found = [VMEM(kept, BF16), VMEM(kept, BF16), VMEM((planes - 1, *once), BF16)]
-    if len(shape) == 5:
-        found += [VMEM(once, BF16), VMEM(once, BF16), VMEM(once, F32)]
-    return found
-
-
-def homing_of(place, wire, grad, home, refs):
-    refs = list(refs)
-    count = 6 if len(grad.shape) == 5 else 3
-    mine, rest = refs[:count], refs[count:]
-    return Homing(place, wire, grad, *mine[:3], mine[3:], home), rest
-
-
 def turn_kernel(
     planes,
-    order, attn, query, key, value, q_unit, k_unit, roots, mixed, lse, wo, cosine, sine, gains,
-    y_out, y_keep, sums_in, grad_g, grad_u, grad_d,
-    d_q, d_k, d_v, grad_o, sums, block_out, home_g, home_u, home_d,
-    d_mixed, attn_sorted, keys_grad, values_grad, y_in, *rest,
+    order, attn_in, query_in, key_in, value_in, q_unit_in, k_unit_in, roots_in, mixed_in, lse_in, wo_in,
+    cosine, sine, gains, y_out, y_keep_in, sums_in, gate_sums, down_sums, grad_u,
+    d_q_out, d_k_out, d_v_out, sums, block_out, home_g, home_u, home_d, home_o,
+    attn, query, key, value, q_unit, k_unit, roots, mixed, lse, wo, y_keep, d_q, d_k, d_v, d_far,
+    d_mixed, attn_sorted, keys_grad, values_grad, y_in, grad_o,
+    g_far, g_leave, g_arrive, g_own, u_came, u_sums, u_far, u_leave, u_arrive, u_own, o_came, o_sums, o_far,
+    out_sems, in_sems, own_sems,
 ):
     p = Place(planes)
-    wire = Wire(*rest[-3:])
-    refs = list(rest[:-3])
+    wire = Wire(out_sems, in_sems, own_sems)
     rows = y_keep.shape[1]
     length = 4 * rows
+    loads = [wire.own(far, near) for far, near in (
+        (attn_in, attn), (wo_in, wo), (mixed_in, mixed), (query_in, query), (key_in, key), (value_in, value),
+        (q_unit_in, q_unit), (k_unit_in, k_unit), (roots_in, roots), (lse_in, lse), (y_keep_in, y_keep))]
     p.meet()
-    homes = []
-    for grad, home in ((grad_d, home_d), (grad_g, home_g), (grad_u, home_u)):
-        one, refs = homing_of(p, wire, grad, home, refs)
-        one.start()
-        homes.append(one)
+    down = Homing(p, wire, False, None, down_sums, d_far, None, home_d)
+    gate = Homing(p, wire, True, None, gate_sums, g_far, (g_leave, g_arrive, g_own), home_g)
+    upper = Homing(p, wire, True, u_came, u_sums, u_far, (u_leave, u_arrive, u_own), home_u)
+    outer = Homing(p, wire, False, o_came, o_sums, o_far, None, home_o)
+    upper.start(grad_u)
+    down.push()
+    gate.push()
+    loads[0].wait()
+    loads[1].wait()
     y_sent = [wire.send(y_out.at[micro], y_in.at[micro], p.x_dev) for micro in range(2)]
 
     def draw(step, carry):
@@ -859,10 +922,13 @@
 
     def out_tile(at, carry):
         cut = pl.ds(pl.multiple_of(at * BLOCK, BLOCK), BLOCK)
-        grad_o[cut] = dot(mixed[:, cut], attn_sorted[...], TALL).astype(BF16)
+        found = dot(mixed[:, cut], attn_sorted[...], TALL).astype(BF16)
+        grad_o[pl.ds(at * (planes // 2), planes // 2)] = found.reshape(planes // 2, *grad_o.shape[1:])
         return carry
 
+    loads[2].wait()
     lax.fori_loop(0, 2, out_tile, 0)
+    outer.start(grad_o)
     sums[...] = sums_in[...]
 
     def lane_of(ref, here, lane):
@@ -921,60 +987,79 @@
         d_v[everything, keys_at] = values_grad[...].astype(BF16)
         return carry
 
+    for copy in loads[3:]:
+        copy.wait()
     lax.fori_loop(0, 1, attend_back, 0)
-    homes[0].spread()
+    upper.add()
+    upper.push()
     lax.fori_loop(1, 2, attend_back, 0)
-    homes[1].spread()
+    outer.add()
+    outer.push()
     for micro in range(2):
         y_sent[micro].wait_recv()
         block_out[micro] = (y_keep[micro] + y_in[micro].astype(F32)).astype(BF16)
-    lax.fori_loop(2, 4, attend_back, 0)
-    homes[2].spread()
-    for one in homes:
-        one.gather()
-    for one in homes:
-        one.finish()
+    def save(micro):
+        half = pl.ds(micro * length, length)
+        return [wire.own(near.at[half], far.at[half]) for near, far in (
+            (d_q, d_q_out), (d_k, d_k_out), (d_v, d_v_out))]
+
+    saved = save(0)
+    lax.fori_loop(2, 3, attend_back, 0)
+    down.gather()
+    gate.gather()
+    lax.fori_loop(3, 4, attend_back, 0)
+    saved += save(1)
+    upper.gather()
+    outer.gather()
+    gate.finish()
+    upper.finish()
+    for copy in saved:
+        copy.wait()
     wire.close()
 
 
 def turn(planes, order, attn, query, key, value, q_unit, k_unit, roots, mixed, lse, wo, cosine, sine, gains,
-         y_out, y_keep, sums, grad_g, grad_u, grad_d):
+         y_out, y_keep, sums, gate_sums, down_sums, grad_u):
     rows = y_keep.shape[1]
     length = 4 * rows
     total = 2 * length
+    out_shape = (planes, 2, 512 // (2 * planes), 1024)
     shapes = [
         jax.ShapeDtypeStruct((total, 512), BF16), jax.ShapeDtypeStruct((total, 256), BF16),
-        jax.ShapeDtypeStruct((total, 256), BF16), jax.ShapeDtypeStruct((512, 1024), BF16),
+        jax.ShapeDtypeStruct((total, 256), BF16),
         jax.ShapeDtypeStruct((8, 1024), F32), jax.ShapeDtypeStruct((2, rows, 1024), BF16),
-        jax.ShapeDtypeStruct((grad_g.shape[3], 4 * grad_g.shape[4]), F32),
         jax.ShapeDtypeStruct((grad_u.shape[3], 4 * grad_u.shape[4]), F32),
-        jax.ShapeDtypeStruct(grad_d.shape[2:], F32),
+        jax.ShapeDtypeStruct((grad_u.shape[3], 4 * grad_u.shape[4]), F32),
+        jax.ShapeDtypeStruct(down_sums.shape[1:], F32), jax.ShapeDtypeStruct(out_shape[2:], F32),
     ]
+    held = (attn, query, key, value, q_unit, k_unit, roots, mixed, lse, wo, y_keep, *shapes[:3])
     vm = pl.BlockSpec(memory_space=VMEM)
     hb = pl.BlockSpec(memory_space=ANY)
     sm = pl.BlockSpec(memory_space=pltpu.SMEM)
     return pl.pallas_call(
         functools.partial(turn_kernel, planes),
         out_shape=shapes,
-        in_specs=[sm] + [vm] * 13 + [hb, vm, vm] + [hb] * 3,
-        out_specs=[vm] * len(shapes),
+        in_specs=[sm] + [hb] * 10 + [vm] * 3 + [hb, hb, vm, vm, vm, hb],
+        out_specs=[hb] * 3 + [vm] * (len(shapes) - 3),
         scratch_shapes=[
+            *[VMEM(item.shape, item.dtype) for item in held], VMEM((planes - 1, *down_sums.shape[1:]), BF16),
             VMEM((total, 512), BF16), VMEM((total, 1024), BF16), VMEM((length, HEAD_DIM), F32),
-            VMEM((length, HEAD_DIM), F32), VMEM((2, rows, 1024), BF16),
-            *homing_scratch(planes, grad_d.shape), *homing_scratch(planes, grad_g.shape),
-            *homing_scratch(planes, grad_u.shape), *wire_scratch(24, 4),
+            VMEM((length, HEAD_DIM), F32), VMEM((2, rows, 1024), BF16), VMEM(out_shape, BF16),
+            *z_scratch(planes, grad_u.shape), *y_scratch(grad_u.shape), *z_scratch(planes, grad_u.shape),
+            *y_scratch(out_shape), *z_scratch(planes, out_shape), *wire_scratch(32, 24),
         ],
         compiler_params=pltpu.CompilerParams(
             collective_id=2, has_side_effects=True, vmem_limit_bytes=VMEM_BYTES),
         name="turn",
     )(order, attn, query, key, value, q_unit, k_unit, roots, mixed, lse, wo, cosine, sine, gains,
-      y_out, y_keep, sums, grad_g, grad_u, grad_d)
+      y_out, y_keep, sums, gate_sums, down_sums, grad_u)
 
 
 def last_kernel(
     planes,
-    rank, normed, d_q, d_k, d_v, wq, wk, wv, tokens, d_resid, gains, sums_in, grad_o,
-    token_grad, sums, home_q, home_k, home_v, home_o,
+    rank, normed_in, d_q_in, d_k_in, d_v_in, wq_in, wk_in, wv_in, tokens, d_resid_in, gains, sums_in,
+    token_grad, sums, home_q, home_k, home_v,
+    normed, d_q, d_k, d_v, wq, wk, wv, d_resid,
     grad_q, grad_k, grad_v, part, sums_out, sums_came,
     core_out, core_in, x_out, x_in, keep, core_s, core_r, x_s, x_r, *rest,
 ):
@@ -985,11 +1070,16 @@
     reducer = Reducer(p, part, core_out, core_in, x_out, x_in, keep, (core_s, core_r, x_s, x_r))
     rows = tokens.shape[1]
     length = 4 * rows
+    loads = [wire.own(far, near) for far, near in (
+        (normed_in, normed), (d_q_in, d_q), (d_k_in, d_k), (d_v_in, d_v), (wq_in, wq), (wk_in, wk), (wv_in, wv),
+        (d_resid_in, d_resid))]
     p.meet()
-    out_home, refs = homing_of(p, wire, grad_o, home_o, refs)
-    out_home.start()
+    loads[0].wait()
     homes = []
-    for grad, pulled, home in ((grad_q, d_q, home_q), (grad_k, d_k, home_k), (grad_v, d_v, home_v)):
+    for grad, pulled, home, load in (
+            (grad_q, d_q, home_q, 1), (grad_k, d_k, home_k, 2), (grad_v, d_v, home_v, 3)):
+        loads[load].wait()
+
         def tile(at, carry, grad=grad, pulled=pulled):
             cut = pl.ds(pl.multiple_of(at * BLOCK, BLOCK), BLOCK)
             found = dot(joined(normed[:, :, cut]), flat(pulled), TALL).astype(BF16)
@@ -997,9 +1087,13 @@
             return carry
 
         lax.fori_loop(0, 4, tile, 0)
-        one, refs = homing_of(p, wire, grad, home, refs)
-        one.start()
+        came, kept, far, *turned = refs[:6]
+        refs = refs[6:]
+        one = Homing(p, wire, True, came, kept, far, turned, home)
+        one.start(grad)
         homes.append(one)
+    for copy in loads[4:]:
+        copy.wait()
     sums[...] = sums_in[...]
 
     def pull(step, carry):
@@ -1015,7 +1109,6 @@
         return carry
 
     lax.fori_loop(0, 8, pull, 0)
-    out_home.spread()
     sums[3:4] = sums[3:4] / gains[0:1]
 
     def exchange(stage, devices, base):
@@ -1033,10 +1126,10 @@
 
     state = exchange(0, (p.core_dev, p.x_dev, p.far_dev), 0)
     for one in homes:
-        one.spread()
+        one.add()
+        one.push()
     absorb(state)
     state = exchange(1, [p.z_dev(step) for step in range(1, planes)], 3)
-    out_home.gather()
     absorb(state)
     state = exchange(2, [p.y_dev], 2 + planes)
     for micro in range(2):
@@ -1055,7 +1148,7 @@
     wire.close()
 
 
-def last(planes, rank, normed, d_q, d_k, d_v, wq, wk, wv, tokens, d_resid, gains, sums, grad_o):
+def last(planes, rank, normed, d_q, d_k, d_v, wq, wk, wv, tokens, d_resid, gains, sums):
     nf = 2 * planes
     rows = tokens.shape[1]
     widths = [wq.shape[1], wk.shape[1], wv.shape[1]]
@@ -1064,26 +1157,26 @@
     shapes = [
         jax.ShapeDtypeStruct((2, rows, 1024), F32), jax.ShapeDtypeStruct((8, 1024), F32),
         *[jax.ShapeDtypeStruct((deep, 4 * wide), F32) for wide in widths],
-        jax.ShapeDtypeStruct(grad_o.shape[2:], F32),
     ]
     vm = pl.BlockSpec(memory_space=VMEM)
+    sm = pl.BlockSpec(memory_space=pltpu.SMEM)
+    held = (normed, d_q, d_k, d_v, wq, wk, wv, d_resid)
+    scratch = [VMEM(item.shape, item.dtype) for item in held] + [VMEM(shape, BF16) for shape in grads]
     hb = pl.BlockSpec(memory_space=ANY)
-    sm = pl.BlockSpec(memory_space=pltpu.SMEM)
-    scratch = [VMEM(shape, BF16) for shape in grads]
     scratch += [VMEM((BLOCK, 1024), F32), VMEM((3, 8, 1024), F32), VMEM((3 + planes, 8, 1024), F32)]
-    scratch += [*reducer_scratch(1024), *homing_scratch(planes, grad_o.shape)]
+    scratch += reducer_scratch(1024)
     for shape in grads:
-        scratch += homing_scratch(planes, shape)
+        scratch += y_scratch(shape) + z_scratch(planes, shape)
     return pl.pallas_call(
         functools.partial(last_kernel, planes),
         out_shape=shapes,
-        in_specs=[sm] + [vm] * 11 + [hb],
+        in_specs=[sm] + [hb] * 7 + [vm, hb, vm, vm],
         out_specs=[vm] * len(shapes),
-        scratch_shapes=scratch + wire_scratch(48, 4),
+        scratch_shapes=scratch + wire_scratch(48, 16),
         compiler_params=pltpu.CompilerParams(
             collective_id=3, has_side_effects=True, vmem_limit_bytes=VMEM_BYTES),
         name="last",
-    )(rank, normed, d_q, d_k, d_v, wq, wk, wv, tokens, d_resid, gains, sums, grad_o)
+    )(rank, normed, d_q, d_k, d_v, wq, wk, wv, tokens, d_resid, gains, sums)
 
 
 def run_tables(positions):
@@ -1115,17 +1208,16 @@
     wq, wk, wv, wo, wg, wu, wd = [
         item.reshape(-1, item.shape[-1]) for item in (wq, wk, wv, wo, wg, wu, wd)]
     post, back = post.reshape(-1, post.shape[-1]), back.reshape(-1, back.shape[-1])
-    grad_g, grad_u, grad_d, y_out, y_keep, d_resid, attn, sums = middle(
+    gate_sums, grad_u, down_sums, y_out, y_keep, d_resid, attn, sums = middle(
         planes, post, back, wg, wu, wd, resid, gains)
     apart = lambda item: item.reshape(-1, RUN, item.shape[-1])
-    columns = lambda item: item.reshape(4, planes, 2, -1, item.shape[-1])
-    lines = lambda item: item.reshape(planes, 2, -1, item.shape[-1])
-    d_q, d_k, d_v, grad_o, sums, block_out, home_g, home_u, home_d = turn(
+    d_q, d_k, d_v, sums, block_out, home_g, home_u, home_d, home_o = turn(
         planes, order, apart(attn), query, key, value, q_unit, k_unit, roots,
         mixed.reshape(-1, mixed.shape[-1]), lse,
-        wo, cosine, sine, gains, y_out, y_keep, sums, columns(grad_g), columns(grad_u), lines(grad_d))
-    token_grad, sums, home_q, home_k, home_v, home_o = last(
-        planes, rank, apart(normed), apart(d_q), apart(d_k), apart(d_v), wq, wk, wv, near, d_resid, gains, sums, lines(grad_o))
+        wo, cosine, sine, gains, y_out, y_keep, sums, gate_sums,
+        down_sums, grad_u)
+    token_grad, sums, home_q, home_k, home_v = last(
+        planes, rank, apart(normed), apart(d_q), apart(d_k), apart(d_v), wq, wk, wv, near, d_resid, gains, sums)
     me = lax.axis_index("seq") * (2 * planes) + lax.axis_index("fsdp")
     small = [
         lax.dynamic_slice(sums, (row, me * item.shape[0]), (1, item.shape[0]))[0]

time: 421 us -> 355 us (0.84)
  Pallas kernels: 401 us -> 335 us
    pallas_call x1, Pallas kernels: 165 us -> 119 us  [front(): pl.pallas_call(functools.partial(front_kernel, planes), out_shape=shapes,...]
    pallas_call x1, Pallas kernels: 70.2 us -> 57 us  [last(): pl.pallas_call(functools.partial(last_kernel, planes), out_shape=shapes,...]
    pallas_call x1, Pallas kernels: 82.9 us -> 71.3 us  [turn(): pl.pallas_call(functools.partial(turn_kernel, planes), out_shape=shapes,...]
    unnamed x38 -> x36, local copies, waits for them, and re-layouts: 7.32 us -> 8.6 us
where the time goes in v3:
time: 355 us; the launch traced here: 352 us
  Pallas kernels  335 us (94%)
  local copies, waits for them, and re-layouts  12.7 us (4%)
  other arithmetic  4.06 us (1%)
    pallas_call x1, Pallas kernels, front(): pl.pallas_call(functools.partial(front_kernel, planes), out_shape=shapes,...  119 us
    pallas_call x1, Pallas kernels, middle(): pl.pallas_call(functools.partial(middle_kernel, planes), out_shape=shapes...  86.9 us
    pallas_call x1, Pallas kernels, turn(): pl.pallas_call(functools.partial(turn_kernel, planes), out_shape=shapes,...  71.3 us
    pallas_call x1, Pallas kernels, last(): pl.pallas_call(functools.partial(last_kernel, planes), out_shape=shapes,...  57 us
    unnamed x36, local copies, waits for them, and re-layouts  8.6 us

profile of v3, /device:TPU:0, one launch (start us, length us, event | category | flops | bytes accessed | tf_op | source)
XLA Modules:
  0.0 352.4 jit_solution(15867203351911750229)
XLA Ops:
  0.7 0.0 copy-start.8
  0.7 0.0 copy-start.9
  0.7 0.0 copy-start.10
  0.7 0.0 copy-start.11
  0.7 0.0 copy-start.12
  0.7 1.9 fusion
  2.6 1.3 pad_maximum_fusion
  3.9 0.0 copy-done.8
  4.0 0.1 slice.3
  4.1 0.1 broadcast_add_fusion
  4.1 0.1 select_reduce_fusion
  4.2 0.1 broadcast_add_fusion.1
  4.3 0.6 add.44.order
  4.9 0.6 fusion.8.gain_tile
  5.5 0.6 reshape.94.rank
  6.1 119.4 %front.1 = (bf16[4,8,32,512]{3,2,1,0:T(8,128)(2,1)}, bf16[4,8,32,256]{3,2,1,0:T(8,128)(2,1)}, bf16[4,8,32,256]{3,2,1,0:T(8,128)(2,1)}, bf16[8,64,1024]{2,1,0:T(8...) custom-call(s32[16]{0:T(128)} %add.44.order, ...), custom_call_target="tpu_custom_call" | custom-call | tf_op jit(solution)/shard_map/front/pallas_call | solution.py:627
  125.5 86.9 %middle.1 = (bf16[4,4,32,768]{3,2,1,0:T(8,128)(2,1)}, bf16[4,4,2,32,768]{4,3,2,1,0:T(8,128)(2,1)}, bf16[4,96,1024]{2,1,0:T(8,128)(2,1)}, bf16[2,256,1024]{2,1,0:...) custom-call(bf16[2048,1024]{1,0:T(8,128)(2,1)} %bitcast.45, ...), custom_call_target="tpu_custom_call" | custom-call | tf_op jit(solution)/shard_map/middle/pallas_call | solution.py:862
  212.4 71.3 %turn.1 = (bf16[2048,512]{1,0:T(8,128)(2,1)}, bf16[2048,256]{1,0:T(8,128)(2,1)}, bf16[2048,256]{1,0:T(8,128)(2,1)}, f32[8,1024]{1,0:T(8,128)}, bf16[2,256,1024]{...) custom-call(s32[16]{0:T(128)} %add.44.order, ...), custom_call_target="tpu_custom_call" | custom-call | tf_op jit(solution)/shard_map/turn/pallas_call | solution.py:1039
  283.7 57.0 %last.1 = (f32[2,256,1024]{2,1,0:T(8,128)}, f32[8,1024]{1,0:T(8,128)}, f32[32,2048]{1,0:T(8,128)}, f32[32,1024]{1,0:T(8,128)}, f32[32,1024]{1,0:T(8,128)}) custom-call(s32[16]{0:T(128)} %reshape.94.rank, bf16[16,128,1024]{2,1,0:T(8,128)(2,1)} %bitcast.43, bf16[16,128,512]{2,1,0:T(8,128)(2,1)} %bitcast.50, bf16[16,128,256]{2,1,0:T(8,128)(2,1)} %bitcast.59, ...), custom_call_target="tpu_custom_call" | custom-call | tf_op jit(solution)/shard_map/last/pallas_call | solution.py:1170
  340.8 0.0 copy-start
  340.8 1.4 dynamic-slice_bitcast_fusion.2
  342.2 1.3 dynamic-slice_bitcast_fusion
  343.6 2.3 copy.43
  345.8 0.0 copy-start.4
  345.8 1.3 copy.44
  347.2 0.7 copy.45
  347.9 0.7 copy.46
  348.5 0.7 copy.47
  349.2 0.7 copy.48
  349.9 0.7 copy.49
  350.7 0.7 copy.50
  351.4 0.7 copy.51
  (24 shorter events, 0.1 us)
Async XLA Ops:
  0.7 3.3 copy-start.8
  0.7 4.2 %copy-start.9 = (bf16[4]{0:T(256)(128)(2,1)S(1)}, bf16[4]{0:T(256)(128)(2,1)}, u32[]{:S(2)}) copy-start(bf16[4]{0:T(256)(128)(2,1)} %param.19) | copy-start | bytes 28
  0.7 4.2 %copy-start.10 = (bf16[4]{0:T(256)(128)(2,1)S(1)}, bf16[4]{0:T(256)(128)(2,1)}, u32[]{:S(2)}) copy-start(bf16[4]{0:T(256)(128)(2,1)} %param.18) | copy-start | bytes 28
  0.7 4.2 %copy-start.11 = (bf16[32]{0:T(256)(128)(2,1)S(1)}, bf16[32]{0:T(256)(128)(2,1)}, u32[]{:S(2)}) copy-start(bf16[32]{0:T(256)(128)(2,1)} %param.17) | copy-start | bytes 196
  0.7 4.2 %copy-start.12 = (bf16[32]{0:T(256)(128)(2,1)S(1)}, bf16[32]{0:T(256)(128)(2,1)}, u32[]{:S(2)}) copy-start(bf16[32]{0:T(256)(128)(2,1)} %param.16) | copy-start | bytes 196
  340.8 5.0 %copy-start = (f32[2,256,1024]{2,1,0:T(8,128)S(1)}, f32[2,256,1024]{2,1,0:T(8,128)}, u32[]{:S(2)}) copy-start(f32[2,256,1024]{2,1,0:T(8,128)} %get-tuple-element.88) | copy-start | bytes 6291460
  345.8 1.4 copy-start.5
  345.8 2.1 copy-start.7
  345.8 2.7 copy-start.6
  345.8 3.4 copy-start.4
  345.8 4.1 %copy-start.3 = (f32[32,3072]{1,0:T(8,128)S(1)}, f32[32,3072]{1,0:T(8,128)}, u32[]{:S(2)}) copy-start(f32[32,3072]{1,0:T(8,128)} %get-tuple-element.161) | copy-start | bytes 1179652
  347.2 3.5 copy-start.2
  347.2 4.2 %copy-start.1 = (f32[96,1024]{1,0:T(8,128)S(1)}, f32[96,1024]{1,0:T(8,128)}, u32[]{:S(2)}) copy-start(f32[96,1024]{1,0:T(8,128)} %get-tuple-element.163) | copy-start | bytes 1179652
